TPU v7x, 256 devices: a whole 4x4x8 slice. The times are simulated.
256 devices in a mesh: tm: 16 (over z_lo, x, core), space: 16 (over z_hi, y).
Axes of the slice: x: 4, y: 4, z: 8 (z_hi: 4, z_lo: 2; z = z_hi * 2 + z_lo), core: 2. Of those that a mesh axis runs over, the one named last changes fastest.
Arguments:
- tokens: bfloat16 [1680, 64, 256], P('space', 'tm'), may hold values from -11 to 11
- w_query: bfloat16 [256, 256], replicated, may hold values from -0.375 to 0.375
- w_key: bfloat16 [256, 256], replicated, may hold values from -0.375 to 0.375
- w_value: bfloat16 [256, 256], replicated, may hold values from -0.375 to 0.375
- w_out: bfloat16 [256, 256], replicated, may hold values from -0.375 to 0.375
- mask: int32 [1680, 1680], P('space'), may hold values from 0 to 1, as said below
- decay: float32 [64, 256], P('tm'), may hold values from 0 to 1
- cotangent: float32 [1680, 64, 256], P('space', 'tm'), may hold values from -6 to 6
Outputs:
- grad_tokens: float32 [1680, 64, 256], P('space', 'tm')
- grad_wq: float32 [256, 256], replicated
- grad_wk: float32 [256, 256], replicated
- grad_wv: float32 [256, 256], replicated
- output_weight_gradient: float32 [256, 256], replicated
Inputs may be any that keep to these rules, and one draw needn't show every extreme that they name: `mask`: every token may attend to itself.
All inputs are finite; a program needn't handle non-finite values.
Results may differ from a plain program's by a relative error of at most 0.03.
The roundings to bfloat16 on the way count: a program that leaves them out, or rounds other values in their place, can miss the bound.
Values may be sent and summed in bfloat16 or wider, within the bound.
A program may use at most 128 MiB of HBM per device.

v0:
```python
import math

import jax
import jax.numpy as jnp
from jax import lax
from jax.sharding import PartitionSpec as P

HEADS = 8


def shifted(array, axis, by):
    devices = lax.axis_size(axis)
    pairs = [(i, i + by) for i in range(devices) if 0 <= i + by < devices]
    return lax.ppermute(array, axis, pairs)


def project(rows_flat, weight):
    return jnp.dot(rows_flat, weight, preferred_element_type=jnp.float32).astype(jnp.bfloat16)


def cross(left, right):
    return lax.dot_general(
        left, right, (((0,), (0,)), ((), ())), preferred_element_type=jnp.float32
    )


def back_project(grads_b, weight):
    return lax.dot_general(
        grads_b, weight, (((1,), (1,)), ((), ())), preferred_element_type=jnp.float32
    )


def shards(tokens, w_query, w_key, w_value, w_out, mask, decay, cotangent):
    tok_rows, round_rows, features = tokens.shape
    head_size = features // HEADS
    score_scale = 1.0 / math.sqrt(head_size)
    x_rounds = jnp.swapaxes(tokens, 0, 1)
    flat_rows = x_rounds.reshape(-1, features)
    queries = project(flat_rows, w_query).reshape(round_rows, tok_rows, HEADS, head_size)
    own_keys = project(flat_rows, w_key).reshape(round_rows, tok_rows, features)
    own_values = project(flat_rows, w_value).reshape(round_rows, tok_rows, features)
    all_keys, all_values = (
        lax.all_gather(own_keys, "space", axis=1, tiled=True),
        lax.all_gather(own_values, "space", axis=1, tiled=True),
    )
    random_key_count = all_keys.shape[1]
    all_keys = all_keys.reshape(round_rows, random_key_count, HEADS, head_size)
    all_values = all_values.reshape(round_rows, random_key_count, HEADS, head_size)
    allowed = mask > 0

    def masked_scores(q_round, k_round):
        scores = (
            jnp.einsum("ihe,jhe->hij", q_round, k_round, preferred_element_type=jnp.float32)
            * score_scale
        )
        return jnp.where(allowed[None], scores, -1e30)

    def forward(round_index):
        scores = masked_scores(queries[round_index], all_keys[round_index])
        maxima = jnp.max(scores, axis=2, keepdims=True)
        expons = jnp.exp(scores - maxima)
        totals = jnp.sum(expons, axis=2, keepdims=True)
        probs_b = (expons / totals).astype(jnp.bfloat16)
        stack_result_matrix = jnp.einsum(
            "hij,jhe->ihe", probs_b, all_values[round_index], preferred_element_type=jnp.float32
        )
        return (stack_result_matrix.astype(jnp.bfloat16), maxima, totals)

    attended, maxima, totals = lax.map(forward, jnp.arange(round_rows))
    local_grads = [None] * round_rows
    reach = [None] * round_rows
    local_grads[round_rows - 1] = cotangent[:, round_rows - 1]
    reach[round_rows - 1] = jnp.ones((1, features), jnp.float32)
    for position in range(round_rows - 2, -1, -1):
        local_grads[position] = (
            cotangent[:, position] + decay[position + 1][None] * local_grads[position + 1]
        )
        reach[position] = decay[position + 1][None] * reach[position + 1]
    block_decay = decay[0][None] * reach[0]
    block_update_message = decay[0][None] * local_grads[0]

    def relay(step_index, state):
        incoming, message = state
        incoming = shifted(message.astype(jnp.bfloat16), "tm", -1).astype(message.dtype)
        return (incoming, block_update_message + block_decay * incoming)

    carried, unused = lax.fori_loop(
        0, lax.axis_size("tm"), relay, (jnp.zeros_like(block_update_message), block_update_message)
    )
    grads = jnp.stack(
        [local_grads[position] + reach[position] * carried for position in range(round_rows)],
        axis=0,
    )
    grads_flat = grads.astype(jnp.bfloat16).reshape(-1, features)
    attended_flat = attended.reshape(-1, features)
    output_weight_gradient = cross(attended_flat, grads_flat)
    upstream = (
        back_project(grads_flat, w_out)
        .astype(jnp.bfloat16)
        .reshape(round_rows, tok_rows, HEADS, head_size)
    )
    deltas = jnp.sum(upstream.astype(jnp.float32) * attended.astype(jnp.float32), axis=3)
    deltas = jnp.swapaxes(deltas, 1, 2)[..., None]

    def backward_round(round_index):
        k_round = all_keys[round_index]
        v_round = all_values[round_index]
        q_round = queries[round_index]
        up_round = upstream[round_index]
        scores = masked_scores(q_round, k_round)
        probs = jnp.exp(scores - maxima[round_index]) / totals[round_index]
        slopes = jnp.einsum("ihe,jhe->hij", up_round, v_round, preferred_element_type=jnp.float32)
        score_grads = (probs * (slopes - deltas[round_index])).astype(jnp.bfloat16)
        grad_query = (
            jnp.einsum("hij,jhe->ihe", score_grads, k_round, preferred_element_type=jnp.float32)
            * score_scale
        )
        grad_key = (
            jnp.einsum("hij,ihe->jhe", score_grads, q_round, preferred_element_type=jnp.float32)
            * score_scale
        )
        grad_value = jnp.einsum(
            "hij,ihe->jhe", probs.astype(jnp.bfloat16), up_round, preferred_element_type=jnp.float32
        )
        partials = jnp.concatenate(
            [
                grad_key.reshape(random_key_count, features),
                grad_value.reshape(random_key_count, features),
            ],
            axis=1,
        )
        partials = partials.astype(jnp.bfloat16).astype(jnp.float32)
        return (grad_query.astype(jnp.bfloat16), partials)

    grad_queries, partial_terms = lax.map(backward_round, jnp.arange(round_rows))
    partial_terms = jnp.swapaxes(partial_terms, 0, 1)
    kv_grads = lax.psum_scatter(
        partial_terms.astype(jnp.bfloat16), "space", scatter_dimension=0, tiled=True
    ).astype(jnp.float32)
    kv_grads = jnp.swapaxes(kv_grads, 0, 1)
    grad_keys = kv_grads[..., :features].astype(jnp.bfloat16).reshape(-1, features)
    grad_values = kv_grads[..., features:].astype(jnp.bfloat16).reshape(-1, features)
    grad_q_flat = grad_queries.reshape(-1, features)
    grad_rows = grads.reshape(-1, features) + back_project(grad_q_flat, w_query)
    grad_rows = grad_rows + back_project(grad_keys, w_key) + back_project(grad_values, w_value)
    grad_tokens = jnp.swapaxes(grad_rows.reshape(round_rows, tok_rows, features), 0, 1)
    summed = lax.psum(
        (
            cross(flat_rows, grad_q_flat),
            cross(flat_rows, grad_keys),
            cross(flat_rows, grad_values),
            output_weight_gradient,
        ),
        ("tm", "space"),
    )
    return (grad_tokens, summed[0], summed[1], summed[2], summed[3])


def solution(mesh):
    return jax.shard_map(
        shards,
        mesh=mesh,
        in_specs=(
            P("space", "tm", None),
            P(),
            P(),
            P(),
            P(),
            P("space", None),
            P("tm", None),
            P("space", "tm", None),
        ),
        out_specs=(P("space", "tm", None), P(), P(), P(), P()),
        check_vma=False,
    )
```

profile of v0, /device:TPU:1, one launch (start us, length us, event | category | flops | bytes accessed | tf_op | source)
XLA Modules:
  0.0 1136.0 jit_solution(881701952524546462)
XLA Ops:
  14.5 124.4 %while.38 = (s32[]{:T(128)}, f32[105,256]{1,0:T(8,128)}, bf16[105,256]{1,0:T(8,128)(2,1)S(1)}, f32[1,256]{1,0:T(1,128)S(1)}, f32[105,256]{1,0:T(8,128)S(1)}, /*index=5*/s32[]{:T(128)}) while((s32[]{:T(128)}, f32[105,256]{1,0:T(8,128)}, bf16[105,256]{1,0:T(8,128)(2,1)S(1)}, f32[1,256]{1,0:T(1,128)S(1)}, f32[105,256]{1,0:T(8,128)S(1)}, ...), condition=%wide.region_1.2_spmd, body=%wide.region_0.1_spmd.sunk | while | flops 107522 | bytes 538733 | solution.py:87
  14.5 5.1 collective-permute-start
  21.6 1.9 collective-permute-start
  23.5 3.6 collective-permute-done
  27.7 1.9 collective-permute-start
  29.6 4.0 collective-permute-done
  34.3 1.9 collective-permute-start
  36.2 3.9 collective-permute-done
  40.8 1.9 collective-permute-start
  42.7 3.6 collective-permute-done
  46.9 1.9 collective-permute-start
  48.8 3.6 collective-permute-done
  53.1 1.9 collective-permute-start
  55.0 4.0 collective-permute-done
  59.6 1.9 collective-permute-start
  61.5 4.0 collective-permute-done
  66.1 1.9 collective-permute-start
  68.1 4.0 collective-permute-done
  72.7 1.9 collective-permute-start
  74.6 4.4 collective-permute-done
  79.7 1.9 collective-permute-start
  81.6 9.1 collective-permute-done
  91.4 1.9 collective-permute-start
  93.3 10.1 collective-permute-done
  104.1 1.9 collective-permute-start
  106.0 5.7 collective-permute-done
  114.3 5.7 collective-permute-done
  122.6 6.1 collective-permute-done
  131.2 7.0 collective-permute-done
  141.6 6.9 copy.82
  148.4 6.1 all-gather.5.cloned.1.call-done
  154.5 6.9 copy.85
  161.5 39.1 %while.39 = (s32[]{:T(128)}, bf16[4,105,8,32]{1,3,2,0:T(8,128)(2,1)S(1)}, f32[4,8,105,1]{2,1,3,0:T(8,128)S(1)}, f32[4,8,105,1]{2,1,3,0:T(8,128)S(1)}, s32[4]{0:T...) while((s32[]{:T(128)}, ...), condition=%wide.region_5.6_spmd, body=%wide.region_2.5_spmd.sunk | while | flops 197593216 | bytes 20291880 | solution.py:69
  164.0 2.6 fusion.96
  168.3 3.0 fusion.98
  173.8 2.6 fusion.96
  178.0 3.0 fusion.98
  183.6 2.6 fusion.96
  187.8 3.0 fusion.98
  193.4 2.6 fusion.96
  197.6 3.0 fusion.98
  200.9 316.6 %while.40 = (s32[]{:T(128)}, bf16[4,105,8,32]{1,3,2,0:T(8,128)(2,1)S(1)}, bf16[4,1680,512]{2,0,1:T(4,128)(2,1)}, s32[4]{0:T(128)S(1)}, bf16[4,1680,8,32]{1,3,2,0...) while((s32[]{:T(128)}, ...), condition=%wide.region_8.9_spmd, body=%wide.region_7.8_spmd.sunk | while | flops 467658240 | bytes 43092636 | solution.py:135
  203.5 3.4 exponential_divide_fusion.2
  207.4 2.3 multiply_convert_fusion.2
  209.7 2.3 fusion.109
  212.8 6.3 copy.148
  219.1 61.0 %dynamic_update_slice.29 = bf16[4,1680,512]{2,0,1:T(4,128)(2,1)} dynamic-update-slice(bf16[4,1680,512]{2,0,1:T(4,128)(2,1)} %get-tuple-element.583, bf16[1,1680,512]{2,0,1:T(2,128)(2,1)} %copy.148, s32[]{:T(128)S(6)} %copy.178, s32[]{:T(128)} %constant.35.clone.1..sunk.1, s32[]{:T(128)} %constant.35.clone.1..sunk.1) | dynamic-update-slice | bytes 3440644 | tf_op jit(solution)/shard_map/while/body/jit(dynamic_update_index_in_dim)/dynamic_update_slice | solution.py:135
  282.6 3.4 exponential_divide_fusion.2
  286.6 2.3 multiply_convert_fusion.2
  288.9 2.3 fusion.109
  291.9 6.3 copy.148
  298.3 61.0 %dynamic_update_slice.29 = bf16[4,1680,512]{2,0,1:T(4,128)(2,1)} dynamic-update-slice(bf16[4,1680,512]{2,0,1:T(4,128)(2,1)} %get-tuple-element.583, bf16[1,1680,512]{2,0,1:T(2,128)(2,1)} %copy.148, s32[]{:T(128)S(6)} %copy.178, s32[]{:T(128)} %constant.35.clone.1..sunk.1, s32[]{:T(128)} %constant.35.clone.1..sunk.1) | dynamic-update-slice | bytes 3440644 | tf_op jit(solution)/shard_map/while/body/jit(dynamic_update_index_in_dim)/dynamic_update_slice | solution.py:135
  361.8 3.4 exponential_divide_fusion.2
  365.7 2.3 multiply_convert_fusion.2
  368.0 2.3 fusion.109
  371.1 6.3 copy.148
  377.4 61.0 %dynamic_update_slice.29 = bf16[4,1680,512]{2,0,1:T(4,128)(2,1)} dynamic-update-slice(bf16[4,1680,512]{2,0,1:T(4,128)(2,1)} %get-tuple-element.583, bf16[1,1680,512]{2,0,1:T(2,128)(2,1)} %copy.148, s32[]{:T(128)S(6)} %copy.178, s32[]{:T(128)} %constant.35.clone.1..sunk.1, s32[]{:T(128)} %constant.35.clone.1..sunk.1) | dynamic-update-slice | bytes 3440644 | tf_op jit(solution)/shard_map/while/body/jit(dynamic_update_index_in_dim)/dynamic_update_slice | solution.py:135
  440.9 3.4 exponential_divide_fusion.2
  444.9 2.3 multiply_convert_fusion.2
  447.1 2.3 fusion.109
  450.2 6.3 copy.148
  456.5 61.0 %dynamic_update_slice.29 = bf16[4,1680,512]{2,0,1:T(4,128)(2,1)} dynamic-update-slice(bf16[4,1680,512]{2,0,1:T(4,128)(2,1)} %get-tuple-element.583, bf16[1,1680,512]{2,0,1:T(2,128)(2,1)} %copy.148, s32[]{:T(128)S(6)} %copy.178, s32[]{:T(128)} %constant.35.clone.1..sunk.1, s32[]{:T(128)} %constant.35.clone.1..sunk.1) | dynamic-update-slice | bytes 3440644 | tf_op jit(solution)/shard_map/while/body/jit(dynamic_update_index_in_dim)/dynamic_update_slice | solution.py:135
  522.9 336.0 %all-reduce.5.cloned.1.call-done = bf16[1680,4,512]{2,1,0:T(4,128)(2,1)} async-done(((bf16[1680,4,512]{2,1,0:T(4,128)(2,1)}), bf16[1680,4,512]{2,1,0:T(4,128)(2,1)}) %all-reduce.5.cloned.1.call-update) | async-done | bytes 6881296
  864.0 258.5 %all-reduce.7.cloned.1.call-done = (f32[256,256]{0,1:T(8,128)}, f32[256,256]{0,1:T(8,128)}, f32[256,256]{0,1:T(8,128)}, f32[256,256]{1,0:T(8,128)}) async-done(((f32[256,256]{0,1:T(8,128)}, f32[256,256]{0,1:T(8,128)}, f32[256,256]{0,1:T(8,128)}, f32[256,256]{1,0:T(8,128)}), (f32[256,256]{0,1:T(8,128)}, f32[256,256]{0,1:T(8,128)}, f32[256,256]{0,1:T(8,128)}, ...) | async-done | bytes 1048592 | tf_op jit(solution)/shard_map/psum | solution.py:147
  (162 shorter events, 60.5 us)
Async XLA Ops:
  7.2 5.5 copy-start
  7.2 7.0 copy-start.16
  7.2 133.5 %copy-start.18 = (bf16[256,256]{1,0:T(8,128)(2,1)S(1)}, bf16[256,256]{1,0:T(8,128)(2,1)}, u32[]{:S(2)}) copy-start(bf16[256,256]{1,0:T(8,128)(2,1)} %param.18) | copy-start | bytes 393220
  7.2 134.4 %all-gather.3.cloned.1.call-start = ((), (), s32[]{:S(2)}) async-start(), calls=%async_computation | async-start | bytes 3655680 | tf_op jit(solution)/shard_map/all_gather | solution.py:43
  8.3 132.8 %copy-start.1 = (bf16[420,256]{1,0:T(8,128)(2,1)}, bf16[420,256]{1,0:T(8,128)(2,1)S(1)}, u32[]{:S(2)}) copy-start(bf16[420,256]{1,0:T(8,128)(2,1)S(1)} %reshape.106) | copy-start | bytes 645124
  10.4 131.0 %copy-start.13 = (s32[105,1680]{1,0:T(8,128)S(1)}, s32[105,1680]{1,0:T(8,128)}, u32[]{:S(2)}) copy-start(s32[105,1680]{1,0:T(8,128)} %param.19) | copy-start | bytes 2116804
  10.4 144.1 %all-gather.5.cloned.1.call-start = ((), (), s32[]{:S(2)}) async-start(), calls=%async_computation.1 | async-start | bytes 3655680 | tf_op jit(solution)/shard_map/all_gather | solution.py:44
  12.6 846.4 %all-reduce.5.cloned.1.call-start = ((), (), s32[]{:S(2)}) async-start(), calls=%async_computation.2 | async-start | bytes 13762560
  14.5 6.4 collective-permute-start
  21.6 5.5 collective-permute-start
  27.7 5.9 collective-permute-start
  34.3 5.8 collective-permute-start
  40.8 5.5 collective-permute-start
  46.9 5.5 collective-permute-start
  53.1 5.9 collective-permute-start
  59.6 5.9 collective-permute-start
  66.1 5.9 collective-permute-start
  72.7 6.3 collective-permute-start
  79.7 11.0 collective-permute-start
  91.4 12.1 %collective-permute-start = (bf16[105,256]{1,0:T(8,128)(2,1)S(1)}, bf16[105,256]{1,0:T(8,128)(2,1)S(1)}, u32[]{:S(2)}, u32[]{:S(2)}) collective-permute-start(bf16[105,256]{1,0:T(8,128)(2,1)S(1)} %get-tuple-element.520), channel_id=1, source_target_pairs={{16,0},{32,16},{48,32},{64,48},{80,64},{96,80},{112,96},{128,112},... | collective-permute-start | bytes 161288 | tf_op jit(solution)/shard_map/while/body/eval_jaxpr/ppermute | solution.py:14
  104.1 7.7 collective-permute-start
  112.4 7.6 collective-permute-start
  120.7 8.0 collective-permute-start
  129.3 8.9 collective-permute-start
  139.9 0.7 copy-start.7
  139.9 0.7 copy-start.9
  139.9 0.7 copy-start.11
  139.9 1.4 copy-start.5
  140.7 20.7 %copy-start.3 = (f32[420,256]{1,0:T(8,128)}, f32[420,256]{1,0:T(8,128)S(1)}, u32[]{:S(2)}) copy-start(f32[420,256]{1,0:T(8,128)S(1)} %reshape.105) | copy-start | bytes 1290244
  517.5 0.9 copy-start.6
  517.5 1.0 copy-start.8
  517.5 1.0 copy-start.10
  517.5 1.1 copy-start.12
  517.5 1.2 copy-start.19
  517.5 3.2 copy-start.2
  517.5 5.1 copy-start.4
  517.6 342.6 %copy-start.17 = (bf16[105,4,256]{2,1,0:T(4,128)(2,1)S(1)}, bf16[105,4,256]{2,1,0:T(4,128)(2,1)}, u32[]{:S(2)}) copy-start(bf16[105,4,256]{2,1,0:T(4,128)(2,1)} %param.14) | copy-start | bytes 645124
  517.6 344.8 %copy-start.14 = (bf16[256,256]{1,0:T(8,128)(2,1)S(1)}, bf16[256,256]{1,0:T(8,128)(2,1)}, u32[]{:S(2)}) copy-start(bf16[256,256]{1,0:T(8,128)(2,1)} %param.16) | copy-start | bytes 393220
  517.6 604.9 %all-reduce.7.cloned.1.call-start = ((), (), s32[]{:S(2)}) async-start(), calls=%async_computation.3 | async-start | bytes 2097152 | tf_op jit(solution)/shard_map/psum | solution.py:147
  518.6 344.0 %copy-start.15 = (bf16[256,256]{1,0:T(8,128)(2,1)S(1)}, bf16[256,256]{1,0:T(8,128)(2,1)}, u32[]{:S(2)}) copy-start(bf16[256,256]{1,0:T(8,128)(2,1)} %param.17) | copy-start | bytes 393220
Sparse Core Ops, SparseCore 0:
  11.0 72.5 all-gather.2
  86.7 67.8 all-gather.4
  517.7 341.1 all-reduce.4
  866.1 256.3 all-reduce.6
where the time goes:
time: 1160 us; the launch traced here: 1140 us
  waiting for transfers between devices  681 us (59%)
  local copies, waits for them, and re-layouts  304 us (26%)
  matrix products  66.1 us (6%)
  starting transfers between devices  34.1 us (3%)
  other arithmetic  20 us (2%)
  loops' own time  16.1 us (1%)
  between operations  15 us (1%)
    unnamed x5, waiting for transfers between devices  336 us
    dynamic_update_slice x8, local copies, waits for them, and re-layouts, shards(): lax.map(backward_round, jnp.arange(round_rows))  269 us
    psum x1, waiting for transfers between devices, shards(): lax.psum((cross(flat_rows, grad_q_flat), cross(flat_rows, grad_keys), cro...  258 us
    ppermute x16, waiting for transfers between devices, shifted(): return lax.ppermute(array, axis, pairs)  79.9 us
    ppermute x16, starting transfers between devices, shifted(): return lax.ppermute(array, axis, pairs)  33.8 us
    dot_general x8, matrix products, masked_scores(): jnp.einsum('ihe,jhe->hij', q_round, k_round, preferred_element_type=jnp.f...  23.9 us
  transfers between devices with their start and end apart: 20, of which 19 were waited for; matrix products, arithmetic and copies ran while one was open for 3% of the time, Pallas kernels for 0%

commit v1 on v0

v1 whole, which is shorter than its diff:
```python
import functools
import math

import jax
import jax.numpy as jnp
from jax import lax
from jax.experimental import pallas as pl
from jax.experimental.pallas import tpu as pltpu
from jax.sharding import PartitionSpec as P

HEADS = 8
NS = 16
NT = 16
NY = 4
MESH = pl.DeviceIdType.MESH
BF = jnp.bfloat16
F32 = jnp.float32
NEG = -1e30
MIB = 1 << 20

VM = pl.BlockSpec(memory_space=pltpu.VMEM)
ANY = pl.BlockSpec(memory_space=pl.ANY)


def params(mib=48, cid=None):
    if cid is None:
        return pltpu.CompilerParams(vmem_limit_bytes=mib * MIB)
    return pltpu.CompilerParams(
        vmem_limit_bytes=mib * MIB, collective_id=cid, has_side_effects=True
    )


def sds(shape, dtype):
    return jax.ShapeDtypeStruct(shape, dtype)


def nt(a, b):
    return lax.dot_general(a, b, (((1,), (1,)), ((), ())), preferred_element_type=F32)


def tn(a, b):
    return lax.dot_general(a, b, (((0,), (0,)), ((), ())), preferred_element_type=F32)


def nn(a, b):
    return jnp.dot(a, b, preferred_element_type=F32)


def mask_kernel(rows, pad, mask_ref, bias_ref):
    groups = NS
    bias_ref[...] = jnp.full(bias_ref.shape, NEG, BF)
    bias = jnp.where(mask_ref[...] > 0, 0.0, NEG).astype(F32)
    for group in range(groups):
        bias_ref[0:rows, group * pad : group * pad + rows] = bias[
            :, group * rows : (group + 1) * rows
        ].astype(BF)


def prep_kernel(x_ref, wq_ref, wk_ref, wv_ref, ct_ref, decay_ref, kv_ref, q_ref, m_ref, d_ref):
    rounds, _, width = x_ref.shape
    for r in range(rounds):
        x = x_ref[r]
        kv_ref[r, :, 0:width] = nn(x, wk_ref[...]).astype(BF)
        kv_ref[r, :, width : 2 * width] = nn(x, wv_ref[...]).astype(BF)
        q_ref[r] = nn(x, wq_ref[...]).astype(BF)
    level = ct_ref[rounds - 1]
    reach = decay_ref[rounds - 1 : rounds, :]
    for r in range(rounds - 2, -1, -1):
        level = ct_ref[r] + decay_ref[r + 1 : r + 2, :] * level
        reach = reach * decay_ref[r : r + 1, :]
    m_ref[...] = (decay_ref[0:1, :] * level).astype(BF)
    d_ref[...] = jnp.broadcast_to(reach, d_ref.shape)


def mid_kernel(ct_ref, decay_ref, m_ref, d_ref, wo_ref, grads_ref, u_ref):
    rounds = ct_ref.shape[0]
    me = lax.axis_index("tm")
    carried = jnp.zeros(ct_ref.shape[1:], F32)
    for k in range(NT - 1, 0, -1):
        inside = me + k < NT
        moved = m_ref[k - 1].astype(F32) + d_ref[k - 1, 0:1, :] * carried
        carried = jnp.where(inside, moved, 0.0)
    level = ct_ref[rounds - 1] + carried
    for r in range(rounds - 1, -1, -1):
        if r < rounds - 1:
            level = ct_ref[r] + decay_ref[r + 1 : r + 2, :] * level
        grads_ref[r] = level
        u_ref[r] = nt(level.astype(BF), wo_ref[...]).astype(BF)


def attention_kernel(
    scale, q_ref, u_ref, kv_ref, bias_ref, qa_ref, dkv_ref,
    kt_ref, vt_ref, qt_ref, ut_ref, s_ref, p_ref, pb_ref, t_ref, ds_ref, acc_q, acc_a, dkt, dvt,
    l_ref,
):
    rows, width = q_ref.shape
    keys = kv_ref.shape[0]
    size = width // HEADS
    kt_ref[...] = kv_ref[:, 0:width].T
    vt_ref[...] = kv_ref[:, width : 2 * width].T
    qt_ref[...] = q_ref[...].T
    ut_ref[...] = u_ref[...].T
    acc_q[...] = jnp.zeros_like(acc_q)
    acc_a[...] = jnp.zeros_like(acc_a)
    chunk = 16

    def head(h, carry):
        own = lax.broadcasted_iota(jnp.int32, (rows, width), 1) // size == h
        here = pl.ds(pl.multiple_of(h * size, size), size)
        qh = jnp.where(own, q_ref[...].astype(F32), 0.0).astype(BF)
        uf = jnp.where(own, u_ref[...].astype(F32), 0.0)
        uh = uf.astype(BF)
        s_ref[...] = nn(qh, kt_ref[...])

        def soft(i, c):
            at = pl.ds(pl.multiple_of(i * chunk, chunk), chunk)
            x = s_ref[at, :] * scale + bias_ref[at, :].astype(F32)
            e = jnp.exp(x - jnp.max(x, axis=1, keepdims=True))
            p = e * (1.0 / jnp.sum(e, axis=1, keepdims=True))
            p_ref[at, :] = p
            pb_ref[at, :] = p.astype(BF)
            return c

        lax.fori_loop(0, rows // chunk, soft, 0)
        a = nn(pb_ref[...], kv_ref[:, width : 2 * width]).astype(BF).astype(F32)
        acc_a[...] = jnp.where(own, a, acc_a[...])
        l_ref[...] = jnp.broadcast_to(jnp.sum(uf * a, axis=1, keepdims=True), l_ref.shape)
        t_ref[...] = nn(uh, vt_ref[...])

        def back(i, c):
            at = pl.ds(pl.multiple_of(i * chunk, chunk), chunk)
            ds_ref[at, :] = (p_ref[at, :] * (t_ref[at, :] - l_ref[at, 0:1])).astype(BF)
            return c

        lax.fori_loop(0, rows // chunk, back, 0)
        acc_q[...] = jnp.where(own, nn(ds_ref[...], kv_ref[:, 0:width]), acc_q[...])
        dkt[here, :] = nn(qt_ref[here, :], ds_ref[...])
        dvt[here, :] = nn(ut_ref[here, :], pb_ref[...])
        return carry

    lax.fori_loop(0, HEADS, head, 0)
    qa_ref[:, 0:width] = (acc_q[...] * scale).astype(BF)
    qa_ref[:, width : 2 * width] = acc_a[...].astype(BF)
    dkv_ref[:, 0:width] = (dkt[...] * scale).T.astype(BF)
    dkv_ref[:, width : 2 * width] = dvt[...].T.astype(BF)


def final_kernel(
    x_ref, grads_ref, qa_ref, part_ref, wq_ref, wk_ref, wv_ref, gt_ref, g_ref
):
    rounds, _, width = x_ref.shape
    half = width // 2
    gq = jnp.zeros((width, width), F32)
    gk, gv, go = gq, gq, gq
    for r in range(rounds):
        total = part_ref[r].astype(F32)
        for z in range(1, NS // NY):
            total = total + part_ref[z * NY + r].astype(F32)
        dk = total[:, 0:width].astype(BF)
        dv = total[:, width : 2 * width].astype(BF)
        dq = qa_ref[r, :, 0:width]
        att = qa_ref[r, :, width : 2 * width]
        grads = grads_ref[r]
        x = x_ref[r]
        gt_ref[r] = grads + nt(dq, wq_ref[...]) + nt(dk, wk_ref[...]) + nt(dv, wv_ref[...])
        gq += tn(x, dq)
        gk += tn(x, dk)
        gv += tn(x, dv)
        go += tn(att, grads.astype(BF))
    for i, g in enumerate((gq, gk, gv, go)):
        g_ref[2 * i] = g[:, 0:half]
        g_ref[2 * i + 1] = g[:, half:width]


def greet(axes):
    barrier = pltpu.get_barrier_semaphore()
    count = 0
    for axis, extent in axes:
        me = lax.axis_index(axis)
        for k in range(1, extent):
            pl.semaphore_signal(
                barrier, inc=1, device_id={axis: lax.rem(me + k, extent)}, device_id_type=MESH
            )
            count += 1
    pl.semaphore_wait(barrier, count)


def push(src, dst, sems, i, axis, to):
    return pltpu.make_async_remote_copy(
        src_ref=src,
        dst_ref=dst,
        send_sem=sems[0].at[i],
        recv_sem=sems[1].at[i],
        device_id={axis: to},
        device_id_type=MESH,
    )


def gather_kernel(
    kv_in, q_in, b_in, m_in, d_in, kv_out, q_out, b_out, m_out, d_out,
    s0, r0, s1, r1, s2, r2, s3, r3, s4, r4, own,
):
    me = lax.axis_index("space")
    y = lax.rem(me, NY)
    base = me - y
    t = lax.axis_index("tm")
    greet((("space", NS), ("tm", NT)))
    copies = []
    for k in range(1, NT):
        for src, dst, sems in ((m_in, m_out, (s3, r3)), (d_in, d_out, (s4, r4))):
            copy = push(src, dst.at[k - 1], sems, k, "tm", jnp.maximum(t - k, 0))
            pl.when(t >= k)(copy.start)
    for k in range(1, NY):
        to = lax.rem(y + k, NY)
        copies.append(push(q_in.at[to], q_out.at[y], (s1, r1), k, "space", base + to))
        copies.append(push(b_in, b_out.at[y], (s2, r2), k, "space", base + to))
    for k in (8, 4, 12, 5, 13, 7, 11, 6, 14, 9, 10, 3, 1, 2, 15):
        to = lax.rem(me + k, NS)
        copies.append(push(kv_in.at[lax.rem(to, NY)], kv_out.at[me], (s0, r0), k, "space", to))
    for copy in copies:
        copy.start()
    locals_ = [
        pltpu.make_async_copy(kv_in.at[y], kv_out.at[me], own.at[0]),
        pltpu.make_async_copy(q_in.at[y], q_out.at[y], own.at[1]),
        pltpu.make_async_copy(b_in, b_out.at[y], own.at[2]),
    ]
    for copy in locals_:
        copy.start()
    for copy in locals_:
        copy.wait()
    for k in range(1, NT):
        for src, dst, sems in ((m_in, m_out, (s3, r3)), (d_in, d_out, (s4, r4))):
            copy = push(src, dst.at[k - 1], sems, k, "tm", jnp.maximum(t - k, 0))
            pl.when(t >= k)(copy.wait_send)
            pl.when(t + k < NT)(copy.wait_recv)
    for copy in copies:
        copy.wait()


def row_kernel(u_in, u_out, s0, r0, own):
    me = lax.axis_index("space")
    y = lax.rem(me, NY)
    base = me - y
    barrier = pltpu.get_barrier_semaphore()
    for k in range(1, NY):
        pl.semaphore_signal(
            barrier, inc=1, device_id={"space": base + lax.rem(y + k, NY)}, device_id_type=MESH
        )
    pl.semaphore_wait(barrier, NY - 1)
    copies = []
    for k in range(1, NY):
        to = lax.rem(y + k, NY)
        copies.append(push(u_in.at[to], u_out.at[y], (s0, r0), k, "space", base + to))
    copies.append(pltpu.make_async_copy(u_in.at[y], u_out.at[y], own))
    for copy in copies:
        copy.start()
    for copy in copies:
        copy.wait()


def scatter_kernel(qa_in, part_in, qa_out, part_out, s0, r0, s1, r1, own):
    me = lax.axis_index("space")
    y = lax.rem(me, NY)
    base = me - y
    greet((("space", NS),))
    copies = []
    for k in (8, 4, 12, 5, 13, 7, 11, 6, 14, 9, 10, 3, 1, 2, 15):
        to = lax.rem(me + k, NS)
        copies.append(push(part_in.at[to], part_out.at[me], (s0, r0), k, "space", to))
    for k in range(1, NY):
        to = lax.rem(y + k, NY)
        copies.append(push(qa_in.at[to], qa_out.at[y], (s1, r1), k, "space", base + to))
    copies.append(pltpu.make_async_copy(part_in.at[me], part_out.at[me], own.at[0]))
    copies.append(pltpu.make_async_copy(qa_in.at[y], qa_out.at[y], own.at[1]))
    for copy in copies:
        copy.start()
    for copy in copies:
        copy.wait()


def reduce_kernel(
    g_in, g_out, send1, got1, part, got2, mine, whole, send4,
    s0, r0, s1, r1, s2, r2, s3, r3,
):
    me = lax.axis_index("space")
    t = lax.axis_index("tm")
    for i in range(NT):
        send1[i] = g_in[i].astype(send1.dtype)
    greet((("space", NS), ("tm", NT)))

    first = []
    for k in range(1, NT):
        to = lax.rem(t + k, NT)
        first.append(push(send1.at[to], got1.at[t], (s0, r0), k, "tm", to))
    for copy in first:
        copy.start()
    total = g_in[t]
    for copy in first:
        copy.wait()
    for k in range(1, NT):
        total = total + got1[lax.rem(t + k, NT)].astype(F32)
    part[...] = total.reshape(part.shape)

    second = []
    for k in range(1, NS):
        to = lax.rem(me + k, NS)
        second.append(push(part.at[to], got2.at[me], (s1, r1), k, "space", to))
    for copy in second:
        copy.start()
    total = part[me]
    for copy in second:
        copy.wait()
    for k in range(1, NS):
        total = total + got2[lax.rem(me + k, NS)]
    mine[...] = total
    whole[me] = total

    third = []
    for k in range(1, NS):
        to = lax.rem(me + k, NS)
        third.append(push(mine, whole.at[me], (s2, r2), k, "space", to))
    for copy in third:
        copy.start()
    for copy in third:
        copy.wait()
    send4[...] = whole[...].reshape(send4.shape).astype(send4.dtype)
    g_out[t] = send4[...]

    fourth = []
    for k in range(1, NT):
        to = lax.rem(t + k, NT)
        fourth.append(push(send4, g_out.at[t], (s3, r3), k, "tm", to))
    for copy in fourth:
        copy.start()
    for copy in fourth:
        copy.wait()


def dma(n):
    return pltpu.SemaphoreType.DMA((n,))


def shards(tokens, w_query, w_key, w_value, w_out, mask, decay, cotangent):
    rows, rounds, width = tokens.shape
    pad = -(-rows // 16) * 16
    keys = NS * pad
    quads = NY * pad
    scale = 1.0 / math.sqrt(width // HEADS)
    size = width // HEADS

    bias = pl.pallas_call(
        functools.partial(mask_kernel, rows, pad),
        out_shape=sds((pad, keys), BF),
        in_specs=[VM],
        out_specs=VM,
        compiler_params=params(),
        name="mask_rows",
    )(mask)
    widen = ((0, 0), (0, pad - rows), (0, 0))
    x = jnp.pad(jnp.swapaxes(tokens, 0, 1), widen)
    ct = jnp.pad(jnp.swapaxes(cotangent, 0, 1), widen)

    kv, q, update, reach = pl.pallas_call(
        prep_kernel,
        out_shape=(
            sds((rounds, pad, 2 * width), BF),
            sds((rounds, pad, width), BF),
            sds((pad, width), BF),
            sds((8, width), F32),
        ),
        in_specs=[VM] * 6,
        out_specs=[VM] * 4,
        compiler_params=params(),
        name="project",
    )(x, w_query, w_key, w_value, ct, decay)

    kv_all, q_all, bias_all, updates, reaches = pl.pallas_call(
        gather_kernel,
        out_shape=(
            sds((NS, pad, 2 * width), BF),
            sds((NY, pad, width), BF),
            sds((NY, pad, keys), BF),
            sds((NT - 1, pad, width), BF),
            sds((NT - 1, 8, width), F32),
        ),
        in_specs=[ANY] * 5,
        out_specs=[ANY] * 5,
        scratch_shapes=[
            dma(NS), dma(NS), dma(NY), dma(NY), dma(NY), dma(NY),
            dma(NT), dma(NT), dma(NT), dma(NT), dma(3),
        ],
        compiler_params=params(cid=1),
        name="gather",
    )(kv, q, bias, update, reach)

    grads, u = pl.pallas_call(
        mid_kernel,
        out_shape=(sds((rounds, pad, width), F32), sds((rounds, pad, width), BF)),
        in_specs=[VM] * 5,
        out_specs=[VM] * 2,
        compiler_params=params(),
        name="recur",
    )(ct, decay, updates, reaches, w_out)

    u_all = pl.pallas_call(
        row_kernel,
        out_shape=sds((NY, pad, width), BF),
        in_specs=[ANY],
        out_specs=ANY,
        scratch_shapes=[dma(NY), dma(NY), pltpu.SemaphoreType.DMA],
        compiler_params=params(cid=2),
        name="upstream_rows",
    )(u)

    qa, dkv = pl.pallas_call(
        functools.partial(attention_kernel, scale),
        out_shape=(sds((quads, 2 * width), BF), sds((keys, 2 * width), BF)),
        in_specs=[VM] * 4,
        out_specs=[VM] * 2,
        scratch_shapes=[
            pltpu.VMEM((width, keys), BF),
            pltpu.VMEM((width, keys), BF),
            pltpu.VMEM((width, quads), BF),
            pltpu.VMEM((width, quads), BF),
            pltpu.VMEM((quads, keys), F32),
            pltpu.VMEM((quads, keys), F32),
            pltpu.VMEM((quads, keys), BF),
            pltpu.VMEM((quads, keys), F32),
            pltpu.VMEM((quads, keys), BF),
            pltpu.VMEM((quads, width), F32),
            pltpu.VMEM((quads, width), F32),
            pltpu.VMEM((width, keys), F32),
            pltpu.VMEM((width, keys), F32),
            pltpu.VMEM((quads, 128), F32),
        ],
        compiler_params=params(56),
        name="attention",
    )(
        q_all.reshape(quads, width),
        u_all.reshape(quads, width),
        kv_all.reshape(keys, 2 * width),
        bias_all.reshape(quads, keys),
    )

    qa_own, parts = pl.pallas_call(
        scatter_kernel,
        out_shape=(sds((NY, pad, 2 * width), BF), sds((NS, pad, 2 * width), BF)),
        in_specs=[ANY] * 2,
        out_specs=[ANY] * 2,
        scratch_shapes=[dma(NS), dma(NS), dma(NY), dma(NY), dma(2)],
        compiler_params=params(cid=3),
        name="scatter",
    )(qa.reshape(NY, pad, 2 * width), dkv.reshape(NS, pad, 2 * width))

    gt, g = pl.pallas_call(
        final_kernel,
        out_shape=(sds((rounds, pad, width), F32), sds((8, width, 128), F32)),
        in_specs=[VM] * 7,
        out_specs=[VM] * 2,
        compiler_params=params(),
        name="finish",
    )(x, grads, qa_own, parts, w_query, w_key, w_value)

    wire = BF
    g = pl.pallas_call(
        reduce_kernel,
        out_shape=sds((NT, 128, 128), wire),
        in_specs=[VM],
        out_specs=VM,
        scratch_shapes=[
            pltpu.VMEM((NT, 128, 128), wire),
            pltpu.VMEM((NT, 128, 128), wire),
            pltpu.VMEM((NS, 8, 128), F32),
            pltpu.VMEM((NS, 8, 128), F32),
            pltpu.VMEM((8, 128), F32),
            pltpu.VMEM((NS, 8, 128), F32),
            pltpu.VMEM((128, 128), wire),
            dma(NT), dma(NT), dma(NS), dma(NS), dma(NS), dma(NS), dma(NT), dma(NT),
        ],
        compiler_params=params(cid=4),
        name="reduce_weights",
    )(g.reshape(NT, 128, 128))
    g = g.astype(F32).reshape(4, 2, width, 128)
    g = jnp.concatenate([g[:, 0], g[:, 1]], axis=2)
    grad_tokens = jnp.swapaxes(gt[:, :rows], 0, 1)
    return (grad_tokens, g[0], g[1], g[2], g[3])


def solution(mesh):
    return jax.shard_map(
        shards,
        mesh=mesh,
        in_specs=(
            P("space", "tm", None),
            P(),
            P(),
            P(),
            P(),
            P("space", None),
            P("tm", None),
            P("space", "tm", None),
        ),
        out_specs=(P("space", "tm", None), P(), P(), P(), P()),
        check_vma=False,
    )
```

time: 1160 us -> 251 us (0.22); the launches traced: 1140 us -> 251 us
  waiting for transfers between devices: 681 us -> 0 us
  local copies, waits for them, and re-layouts: 304 us -> 9.13 us
  Pallas kernels: 0 us -> 240 us
  matrix products: 66.1 us -> 0 us
  starting transfers between devices: 34.1 us -> 0 us
  other arithmetic: 20 us -> 1.05 us
  loops' own time: 16.1 us -> 0 us
  between operations: 15 us -> 0.86 us
    unnamed x5 -> x0, waiting for transfers between devices: 336 us -> none
    dynamic_update_slice x12 -> x0, local copies, waits for them, and re-layouts: 269 us -> none  [the longest x8 269 us: shards(): lax.map(backward_round, jnp.arange(round_rows))]
    psum x1 -> x0, waiting for transfers between devices: 258 us -> none  [shards(): lax.psum((cross(flat_rows, grad_q_flat), cross(flat_rows, grad_keys), cro...]
    pallas_call x0 -> x9, Pallas kernels: none -> 240 us  [the longest x1 90.9 us: shards(): pl.pallas_call(functools.partial(attention_kernel, scale), out_shape=(sds...]
    ppermute x16 -> x0, waiting for transfers between devices: 79.9 us -> none  [shifted(): return lax.ppermute(array, axis, pairs)]
    dot_general x39 -> x0, matrix products: 66.1 us -> none  [the longest x8 23.9 us: masked_scores(): jnp.einsum('ihe,jhe->hij', q_round, k_round, preferred_element_type=jnp.f...]
    ppermute x16 -> x0, starting transfers between devices: 33.8 us -> none  [shifted(): return lax.ppermute(array, axis, pairs)]
    another operation x3 -> x0, loops' own time: 16.1 us -> none  [the longest x1 8.02 us: shards(): lax.map(backward_round, jnp.arange(round_rows))]
  transfers between devices with their start and end apart: 20 -> 0, of which waited for: 19 -> 0; matrix products, arithmetic and copies ran while one was open for 3% -> 0% of each run, Pallas kernels for 0% -> 0%
where the time goes in v1:
time: 251 us
  Pallas kernels  240 us (96%)
  local copies, waits for them, and re-layouts  9.13 us (4%)
    pallas_call x1, Pallas kernels, shards(): pl.pallas_call(functools.partial(attention_kernel, scale), out_shape=(sds...  90.9 us
    pallas_call x1, Pallas kernels, shards(): pl.pallas_call(gather_kernel, out_shape=(sds((NS, pad, 2 * width), BF), s...  54.8 us
    pallas_call x1, Pallas kernels, shards(): pl.pallas_call(reduce_kernel, out_shape=sds((NT, 128, 128), wire), in_spe...  51.4 us
    pallas_call x1, Pallas kernels, shards(): pl.pallas_call(scatter_kernel, out_shape=(sds((NY, pad, 2 * width), BF),...  35 us
    unnamed x29, local copies, waits for them, and re-layouts  8.98 us
    pallas_call x1, Pallas kernels, shards(): pl.pallas_call(row_kernel, out_shape=sds((NY, pad, width), BF), in_specs=...  5.4 us

profile of v1, /device:TPU:1, one launch (start us, length us, event | category | flops | bytes accessed | tf_op | source)
XLA Modules:
  0.0 250.8 jit_solution(2689719354996583858)
XLA Ops:
  0.6 0.0 copy-start.12
  0.6 1.0 copy.23
  1.7 0.0 copy-start.5
  1.7 0.0 copy-start.6
  1.7 0.0 copy-start.7
  1.7 0.0 copy-start.11
  1.7 0.0 copy-start.4
  1.7 1.2 copy-done.4
  2.9 0.3 mask_rows.1.b_in
  3.2 0.0 copy-done.12
  3.3 0.0 copy-start.10
  3.3 0.1 copy.22
  3.4 0.0 copy-done.5
  3.4 0.0 copy-done.6
  3.4 0.0 copy-done.7
  3.4 0.0 copy-done.11
  3.4 0.4 project.1
  3.8 54.8 %gather.1 = (bf16[16,112,512]{2,1,0:T(8,128)(2,1)S(1)}, bf16[4,112,256]{2,1,0:T(8,128)(2,1)S(1)}, bf16[4,112,1792]{2,1,0:T(8,128)(2,1)S(1)}, bf16[15,112,256]{2,1,0:T(8,128)(2,1)S(1)}, f32[15,8,256]{2,1,0:T(8,128)S(1)}) custom-call(bf16[4,112,512]{2,1,0:T(8,128)(2,1)S(1)} %get-tuple-element.22.kv_in, bf16[4,112,256]{2,1,0:T(8,128)(2,1)S(1)} %get-tuple-element.23.q_in, ...), custom_call_target="tpu_custom_call" | custom-call | tf_op jit(solution)/shard_map/gather/pallas_call | solution.py:377
  58.6 0.0 copy-start
  58.6 1.2 copy-done
  59.8 0.0 copy-start.2
  59.9 1.2 copy-done.2
  61.0 0.0 copy-start.9
  61.0 0.0 copy-done.10
  61.0 0.5 recur.1
  61.5 5.4 %upstream_rows.1 = bf16[4,112,256]{2,1,0:T(8,128)(2,1)S(1)} custom-call(bf16[4,112,256]{2,1,0:T(8,128)(2,1)S(1)} %get-tuple-element.30.u_in), custom_call_target="tpu_custom_call" | custom-call | tf_op jit(solution)/shard_map/upstream_rows/pallas_call | solution.py:405
  66.9 0.0 copy-done.9
  66.9 0.0 copy-start.3
  66.9 0.7 copy-done.3
  67.6 90.9 %attention.1 = (bf16[448,512]{1,0:T(8,128)(2,1)}, bf16[1792,512]{1,0:T(8,128)(2,1)}) custom-call(bf16[448,256]{1,0:T(8,128)(2,1)} %bitcast.40, bf16[448,256]{1,0:T(8,128)(2,1)} %bitcast.38, bf16[1792,512]{1,0:T(8,128)(2,1)} %bitcast.34, bf16[448,1792]{1,0:T(8,128)(2,1)} %bitcast.36), custom_call_target="tpu_custom_call" | custom-call | tf_op jit(solution)/shard_map/attention/pallas_call | solution.py:415
  158.5 0.0 copy-start.1
  158.5 1.5 copy-done.1
  160.0 0.0 copy-start.8
  160.0 1.0 copy-done.8
  161.0 35.0 %scatter.1 = (bf16[4,112,512]{2,1,0:T(8,128)(2,1)S(1)}, bf16[16,112,512]{2,1,0:T(8,128)(2,1)S(1)}) custom-call(bf16[4,112,512]{2,1,0:T(8,128)(2,1)S(1)} %bitcast.39, bf16[16,112,512]{2,1,0:T(8,128)(2,1)S(1)} %bitcast.35), custom_call_target="tpu_custom_call" | custom-call | tf_op jit(solution)/shard_map/scatter/pallas_call | solution.py:445
  196.0 1.1 finish.1
  197.2 1.0 copy.17
  198.2 51.4 %reduce_weights.1 = bf16[16,128,128]{2,1,0:T(8,128)(2,1)S(1)} custom-call(f32[16,128,128]{2,1,0:T(8,128)S(1)} %bitcast.37), custom_call_target="tpu_custom_call" | custom-call | tf_op jit(solution)/shard_map/reduce_weights/pallas_call | solution.py:465
  249.7 0.1 convert.1
  249.7 0.1 slice_bitcast_fusion
  249.8 1.0 fusion.6
  (3 shorter events, 0.1 us)
Async XLA Ops:
  0.6 2.6 %copy-start.12 = (f32[105,4,256]{2,1,0:T(4,128)S(1)}, f32[105,4,256]{2,1,0:T(4,128)}, u32[]{:S(2)}) copy-start(f32[105,4,256]{2,1,0:T(4,128)} %param.15) | copy-start | bytes 1290244
  1.7 1.8 copy-start.5
  1.7 1.8 copy-start.6
  1.7 1.7 copy-start.7
  1.7 1.7 copy-start.11
  1.7 1.2 copy-start.4
  3.3 57.8 %copy-start.10 = (bf16[256,256]{1,0:T(8,128)(2,1)S(1)}, bf16[256,256]{1,0:T(8,128)(2,1)}, u32[]{:S(2)}) copy-start(bf16[256,256]{1,0:T(8,128)(2,1)} %wo_ref.1) | copy-start | bytes 393220
  58.6 1.2 copy-start
  59.8 1.2 copy-start.2
  61.0 5.9 %copy-start.9 = (bf16[4,112,256]{2,1,0:T(8,128)(2,1)}, bf16[4,112,256]{2,1,0:T(8,128)(2,1)S(1)}, u32[]{:S(2)}) copy-start(bf16[4,112,256]{2,1,0:T(8,128)(2,1)S(1)} %get-tuple-element.29) | copy-start | bytes 688132
  66.9 0.7 copy-start.3
  158.5 1.5 copy-start.1
  160.0 1.0 copy-start.8

commit v2 on v1

v2 whole, which is shorter than its diff:
```python
import functools
import math

import jax
import jax.numpy as jnp
from jax import lax
from jax.experimental import pallas as pl
from jax.experimental.pallas import tpu as pltpu
from jax.sharding import PartitionSpec as P

HEADS = 8
NS = 16
NT = 16
NY = 4
MESH = pl.DeviceIdType.MESH
BF = jnp.bfloat16
F32 = jnp.float32
NEG = -1e30
MIB = 1 << 20

VM = pl.BlockSpec(memory_space=pltpu.VMEM)
ANY = pl.BlockSpec(memory_space=pl.ANY)


def params(mib=48, cid=None):
    if cid is None:
        return pltpu.CompilerParams(vmem_limit_bytes=mib * MIB)
    return pltpu.CompilerParams(
        vmem_limit_bytes=mib * MIB, collective_id=cid, has_side_effects=True
    )


def sds(shape, dtype):
    return jax.ShapeDtypeStruct(shape, dtype)


def nt(a, b):
    return lax.dot_general(a, b, (((1,), (1,)), ((), ())), preferred_element_type=F32)


def tn(a, b):
    return lax.dot_general(a, b, (((0,), (0,)), ((), ())), preferred_element_type=F32)


def nn(a, b):
    return jnp.dot(a, b, preferred_element_type=F32)


def mask_kernel(rows, pad, mask_ref, bias_ref):
    bias_ref[...] = jnp.full(bias_ref.shape, NEG, BF)
    bias = jnp.where(mask_ref[...] > 0, 0.0, NEG).astype(F32)
    for group in range(NS):
        bias_ref[0:rows, group * pad : group * pad + rows] = bias[
            :, group * rows : (group + 1) * rows
        ].astype(BF)


def attention_kernel(
    scale, x_ref, gb_ref, bias_ref, wq_ref, wk_ref, wv_ref, wo_ref, c_ref, g_ref,
    k_ref, v_ref, kt_ref, vt_ref, qt_ref, u_ref, ut_ref, q32, u32,
    s_ref, p_ref, pb_ref, t_ref, ds_ref, acc_q, acc_a, dkt, dvt,
):
    rows, width = gb_ref.shape
    size = width // HEADS
    half = width // 2
    first = pl.multiple_of(lax.axis_index("space") // NY * rows, rows)
    x = x_ref[...]
    xq = x_ref[pl.ds(first, rows), :]
    k_ref[...] = nn(x, wk_ref[...]).astype(BF)
    v_ref[...] = nn(x, wv_ref[...]).astype(BF)
    kt_ref[...] = nt(wk_ref[...].T, x).astype(BF)
    vt_ref[...] = nt(wv_ref[...].T, x).astype(BF)
    q = nn(xq, wq_ref[...]).astype(BF)
    qt_ref[...] = nt(wq_ref[...].T, xq).astype(BF)
    u_ref[...] = nt(gb_ref[...], wo_ref[...]).astype(BF)
    ut_ref[...] = nt(wo_ref[...], gb_ref[...]).astype(BF)
    for h in range(HEADS):
        q32[h] = q[:, h * size : (h + 1) * size]
        u32[h] = u_ref[:, h * size : (h + 1) * size]
    acc_q[...] = jnp.zeros_like(acc_q)
    acc_a[...] = jnp.zeros_like(acc_a)
    block, step = rows // 2, 16
    blocks = rows // block

    def head(h, carry):
        here = pl.ds(pl.multiple_of(h * size, size), size)
        own = lax.broadcasted_iota(jnp.int32, (block, width), 1) // size == h

        def scores(b):
            at = pl.ds(b * block, block)
            s_ref[at] = nn(q32[h, at, :], kt_ref[here, :])

        def slopes(b):
            at = pl.ds(b * block, block)
            t_ref[at] = nn(u32[h, at, :], vt_ref[here, :])

        def softmax(b):
            for i in range(block // step):
                at = pl.ds(b * block + i * step, step)
                z = s_ref[at, :] * scale + bias_ref[at, :].astype(F32)
                e = jnp.exp(z - jnp.max(z, axis=1, keepdims=True))
                p = e * (1.0 / jnp.sum(e, axis=1, keepdims=True))
                p_ref[at, :] = p
                pb_ref[at, :] = p.astype(BF)

        def attend(b):
            at = pl.ds(b * block, block)
            a = nn(pb_ref[at], v_ref[...]).astype(BF).astype(F32)
            a = jnp.where(own, a, 0.0)
            acc_a[at] += a
            return jnp.sum(u_ref[at].astype(F32) * a, axis=1, keepdims=True)

        def score_grads(b, deltas):
            for i in range(block // step):
                at = pl.ds(b * block + i * step, step)
                ds_ref[at, :] = (
                    p_ref[at, :] * (t_ref[at, :] - deltas[i * step : (i + 1) * step])
                ).astype(BF)
            at = pl.ds(b * block, block)
            acc_q[at] += jnp.where(own, nn(ds_ref[at], k_ref[...]), 0.0)

        scores(0)
        deltas = None
        for b in range(blocks):
            if b + 1 < blocks:
                scores(b + 1)
            slopes(b)
            softmax(b)
            if b > 0:
                score_grads(b - 1, deltas)
            deltas = attend(b)
        score_grads(blocks - 1, deltas)
        dkt[here, :] = nn(qt_ref[here, :], ds_ref[...])
        dvt[here, :] = nn(ut_ref[here, :], pb_ref[...])
        return carry

    lax.fori_loop(0, HEADS, head, 0)
    dq = (acc_q[...] * scale).astype(BF)
    dk = (dkt[...] * scale).astype(BF)
    dv = dvt[...].astype(BF)
    c_ref[...] = (nn(wk_ref[...], dk) + nn(wv_ref[...], dv)).T.astype(BF)
    own_rows = pl.ds(first, rows)
    back = nt(dq, wq_ref[...])
    c_ref[own_rows, :] = (c_ref[own_rows, :].astype(F32) + back).astype(BF)
    weights = (
        tn(xq, dq),
        nn(dk, x).T,
        nn(dv, x).T,
        tn(acc_a[...].astype(BF), gb_ref[...]),
    )
    for i, g in enumerate(weights):
        g_ref[2 * i] = g[:, 0:half]
        g_ref[2 * i + 1] = g[:, half:width]


SPREAD = (8, 4, 12, 5, 13, 7, 11, 6, 14, 9, 10, 3, 1, 2, 15)


def greet(axes):
    barrier = pltpu.get_barrier_semaphore()
    count = 0
    for axis, extent in axes:
        me = lax.axis_index(axis)
        for k in range(1, extent):
            pl.semaphore_signal(
                barrier, inc=1, device_id={axis: lax.rem(me + k, extent)}, device_id_type=MESH
            )
            count += 1
    pl.semaphore_wait(barrier, count)


def push(src, dst, sems, i, axis, to):
    return pltpu.make_async_remote_copy(
        src_ref=src,
        dst_ref=dst,
        send_sem=sems[0].at[i],
        recv_sem=sems[1].at[i],
        device_id={axis: to},
        device_id_type=MESH,
    )


def gather_kernel(
    x_in, b_in, ct_ref, decay_ref, x_out, b_out, gb_out, grads_ref,
    m_send, d_send, m_got, d_got, gb_send, carried,
    s0, r0, s1, r1, s2, r2, s3, r3, s4, r4, s5, r5, own,
):
    rounds = ct_ref.shape[0]
    cols = b_in.shape[1] // 2
    me = lax.axis_index("space")
    y = lax.rem(me, NY)
    base = me - y
    t = lax.axis_index("tm")
    core = lax.rem(t, 2)
    half = pl.ds(pl.multiple_of(core * cols, cols), cols)

    level = ct_ref[rounds - 1]
    reach = decay_ref[rounds - 1 : rounds, :]
    for r in range(rounds - 2, -1, -1):
        level = ct_ref[r] + decay_ref[r + 1 : r + 2, :] * level
        reach = reach * decay_ref[r : r + 1, :]
    m_send[...] = (decay_ref[0:1, :] * level).astype(BF)
    d_send[...] = jnp.broadcast_to(reach, d_send.shape)

    greet((("tm", NT), ("space", NS)))
    for k in range(1, NT):
        to = jnp.maximum(t - k, 0)
        pl.when(t >= k)(push(m_send, m_got.at[k - 1], (s3, r3), k, "tm", to).start)
        pl.when(t >= k)(push(d_send, d_got.at[k - 1], (s4, r4), k, "tm", to).start)
    tokens = []
    for k in SPREAD:
        to = lax.rem(me + k, NS)
        tokens.append(push(x_in.at[lax.rem(to, NY)], x_out.at[me], (s0, r0), k, "space", to))
    masks = []
    for k in range(1, NY):
        to = lax.rem(y + k, NY)
        masks.append(
            push(b_in.at[:, half], b_out.at[y, :, half], (s2, r2), k, "space", base + to)
        )
    local = [
        pltpu.make_async_copy(x_in.at[y], x_out.at[me], own.at[0]),
        pltpu.make_async_copy(b_in, b_out.at[y], own.at[1]),
    ]
    for copy in masks + tokens + local:
        copy.start()

    for k in range(1, NT):
        to = jnp.maximum(t - k, 0)
        for src, dst, sems in ((m_send, m_got, (s3, r3)), (d_send, d_got, (s4, r4))):
            copy = push(src, dst.at[k - 1], sems, k, "tm", to)
            pl.when(t + k < NT)(copy.wait_recv)
    carried[...] = jnp.zeros(carried.shape, F32)
    for k in range(NT - 1, 0, -1):

        @pl.when(t + k < NT)
        def _():
            carried[...] = m_got[k - 1].astype(F32) + d_got[k - 1, 0:1, :] * carried[...]

    level = ct_ref[rounds - 1] + carried[...]
    for r in range(rounds - 1, -1, -1):
        if r < rounds - 1:
            level = ct_ref[r] + decay_ref[r + 1 : r + 2, :] * level
        grads_ref[r] = level
        gb_send[r] = level.astype(BF)
    ups = []
    for k in range(1, NY):
        to = lax.rem(y + k, NY)
        ups.append(push(gb_send.at[to], gb_out.at[y], (s1, r1), k, "space", base + to))
    ups.append(pltpu.make_async_copy(gb_send.at[y], gb_out.at[y], own.at[2]))
    for copy in ups:
        copy.start()

    shared = []
    for k in range(1, NY):
        masks[k - 1].wait()
        src = lax.rem(y - k + NY, NY)
        copy = push(
            b_out.at[src, :, half], b_out.at[src, :, half], (s5, r5), k, "tm", t + 1 - 2 * core
        )
        copy.start()
        shared.append(copy)
    for k in range(1, NT):
        to = jnp.maximum(t - k, 0)
        for src, dst, sems in ((m_send, m_got, (s3, r3)), (d_send, d_got, (s4, r4))):
            pl.when(t >= k)(push(src, dst.at[k - 1], sems, k, "tm", to).wait_send)
    for copy in tokens + local + ups + shared:
        copy.wait()


def scatter_kernel(
    c_in, g_in, c_out, g_out, send1, got1, part, got2, mine, whole, send4,
    s0, r0, s1, r1, s2, r2, s3, r3, s4, r4, own,
):
    me = lax.axis_index("space")
    t = lax.axis_index("tm")
    for i in range(NT):
        send1[i] = g_in[i].astype(send1.dtype)
    greet((("tm", NT), ("space", NS)))

    first = []
    for k in range(1, NT):
        to = lax.rem(t + k, NT)
        first.append(push(send1.at[to], got1.at[t], (s0, r0), k, "tm", to))
    tokens = []
    for k in SPREAD:
        to = lax.rem(me + k, NS)
        tokens.append(push(c_in.at[to], c_out.at[me], (s4, r4), k, "space", to))
    tokens.append(pltpu.make_async_copy(c_in.at[me], c_out.at[me], own))
    for copy in first + tokens:
        copy.start()
    total = g_in[t]
    for copy in first:
        copy.wait()
    for k in range(1, NT):
        total = total + got1[lax.rem(t + k, NT)].astype(F32)
    part[...] = total.reshape(part.shape)

    second = []
    for k in range(1, NS):
        to = lax.rem(me + k, NS)
        second.append(push(part.at[to], got2.at[me], (s1, r1), k, "space", to))
    for copy in second:
        copy.start()
    total = part[me]
    for copy in second:
        copy.wait()
    for k in range(1, NS):
        total = total + got2[lax.rem(me + k, NS)]
    mine[...] = total
    whole[me] = total

    third = []
    for k in range(1, NS):
        to = lax.rem(me + k, NS)
        third.append(push(mine, whole.at[me], (s2, r2), k, "space", to))
    for copy in third:
        copy.start()
    for copy in third:
        copy.wait()
    send4[...] = whole[...].reshape(send4.shape).astype(send4.dtype)
    g_out[t] = send4[...]

    fourth = []
    for k in range(1, NT):
        to = lax.rem(t + k, NT)
        fourth.append(push(send4, g_out.at[t], (s3, r3), k, "tm", to))
    for copy in fourth:
        copy.start()
    for copy in fourth + tokens:
        copy.wait()


def dma(n):
    return pltpu.SemaphoreType.DMA((n,))


def shards(tokens, w_query, w_key, w_value, w_out, mask, decay, cotangent):
    rows, rounds, width = tokens.shape
    pad = -(-rows // 16) * 16
    keys = NS * pad
    quads = NY * pad
    size = width // HEADS
    scale = 1.0 / math.sqrt(size)

    bias = pl.pallas_call(
        functools.partial(mask_kernel, rows, pad),
        out_shape=sds((pad, keys), BF),
        in_specs=[VM],
        out_specs=VM,
        compiler_params=params(),
        name="mask_rows",
    )(mask)
    widen = ((0, 0), (0, pad - rows), (0, 0))
    x = jnp.pad(jnp.swapaxes(tokens, 0, 1), widen)
    ct = jnp.pad(jnp.swapaxes(cotangent, 0, 1), widen)

    x_all, bias_all, gb_all, grads = pl.pallas_call(
        gather_kernel,
        out_shape=(
            sds((NS, pad, width), BF),
            sds((NY, pad, keys), BF),
            sds((NY, pad, width), BF),
            sds((rounds, pad, width), F32),
        ),
        in_specs=[ANY, ANY, VM, VM],
        out_specs=[ANY, ANY, ANY, VM],
        scratch_shapes=[
            pltpu.VMEM((pad, width), BF),
            pltpu.VMEM((8, width), F32),
            pltpu.VMEM((NT - 1, pad, width), BF),
            pltpu.VMEM((NT - 1, 8, width), F32),
            pltpu.VMEM((rounds, pad, width), BF),
            pltpu.VMEM((pad, width), F32),
            dma(NS), dma(NS), dma(NY), dma(NY), dma(NY), dma(NY),
            dma(NT), dma(NT), dma(NT), dma(NT), dma(NY), dma(NY), dma(3),
        ],
        compiler_params=params(cid=1),
        name="gather",
    )(x, bias, ct, decay)

    c, g = pl.pallas_call(
        functools.partial(attention_kernel, scale),
        out_shape=(sds((keys, width), BF), sds((8, width, width // 2), F32)),
        in_specs=[VM] * 7,
        out_specs=[VM] * 2,
        scratch_shapes=[
            pltpu.VMEM((keys, width), BF),
            pltpu.VMEM((keys, width), BF),
            pltpu.VMEM((width, keys), BF),
            pltpu.VMEM((width, keys), BF),
            pltpu.VMEM((width, quads), BF),
            pltpu.VMEM((quads, width), BF),
            pltpu.VMEM((width, quads), BF),
            pltpu.VMEM((HEADS, quads, size), BF),
            pltpu.VMEM((HEADS, quads, size), BF),
            pltpu.VMEM((quads, keys), F32),
            pltpu.VMEM((quads, keys), F32),
            pltpu.VMEM((quads, keys), BF),
            pltpu.VMEM((quads, keys), F32),
            pltpu.VMEM((quads, keys), BF),
            pltpu.VMEM((quads, width), F32),
            pltpu.VMEM((quads, width), F32),
            pltpu.VMEM((width, keys), F32),
            pltpu.VMEM((width, keys), F32),
        ],
        compiler_params=params(58),
        name="attention",
    )(
        x_all.reshape(keys, width),
        gb_all.reshape(quads, width),
        bias_all.reshape(quads, keys),
        w_query, w_key, w_value, w_out,
    )

    wire = BF
    parts, g = pl.pallas_call(
        scatter_kernel,
        out_shape=(sds((NS, pad, width), BF), sds((NT, 128, 128), wire)),
        in_specs=[ANY, VM],
        out_specs=[ANY, VM],
        scratch_shapes=[
            pltpu.VMEM((NT, 128, 128), wire),
            pltpu.VMEM((NT, 128, 128), wire),
            pltpu.VMEM((NS, 8, 128), F32),
            pltpu.VMEM((NS, 8, 128), F32),
            pltpu.VMEM((8, 128), F32),
            pltpu.VMEM((NS, 8, 128), F32),
            pltpu.VMEM((128, 128), wire),
            dma(NT), dma(NT), dma(NS), dma(NS), dma(NS), dma(NS), dma(NT), dma(NT),
            dma(NS), dma(NS), pltpu.SemaphoreType.DMA,
        ],
        compiler_params=params(cid=2),
        name="scatter",
    )(c.reshape(NS, pad, width), g.reshape(NT, 128, 128))
    parts = parts.reshape(NS // NY, rounds, pad, width)
    gt = grads + sum(parts[z].astype(F32) for z in range(NS // NY))
    g = g.astype(F32).reshape(4, 2, width, 128)
    g = jnp.concatenate([g[:, 0], g[:, 1]], axis=2)
    grad_tokens = jnp.swapaxes(gt[:, :rows], 0, 1)
    return (grad_tokens, g[0], g[1], g[2], g[3])


def solution(mesh):
    return jax.shard_map(
        shards,
        mesh=mesh,
        in_specs=(
            P("space", "tm", None),
            P(),
            P(),
            P(),
            P(),
            P("space", None),
            P("tm", None),
            P("space", "tm", None),
        ),
        out_specs=(P("space", "tm", None), P(), P(), P(), P()),
        check_vma=False,
    )
```

time: 251 us -> 138 us (0.55)
  Pallas kernels: 240 us -> 127 us
    pallas_call x1, Pallas kernels: 90.9 us -> 29.5 us  [shards(): pl.pallas_call(functools.partial(attention_kernel, scale), out_shape=(sds...]
    pallas_call x7 -> x2, Pallas kernels: 149 us -> 96.7 us  [the longest x1 59.8 us: shards(): pl.pallas_call(scatter_kernel, out_shape=(sds((NS, pad, width), BF), sds(...]
    unnamed x29 -> x19, local copies, waits for them, and re-layouts: 8.98 us -> 8.68 us
where the time goes in v2:
time: 138 us; the launch traced here: 137 us
  Pallas kernels  127 us (92%)
  local copies, waits for them, and re-layouts  8.86 us (6%)
    pallas_call x1, Pallas kernels, shards(): pl.pallas_call(scatter_kernel, out_shape=(sds((NS, pad, width), BF), sds(...  59.8 us
    pallas_call x1, Pallas kernels, shards(): pl.pallas_call(gather_kernel, out_shape=(sds((NS, pad, width), BF), sds((...  36.9 us
    pallas_call x1, Pallas kernels, shards(): pl.pallas_call(functools.partial(attention_kernel, scale), out_shape=(sds...  29.5 us
    unnamed x19, local copies, waits for them, and re-layouts  8.68 us

profile of v2, /device:TPU:1, one launch (start us, length us, event | category | flops | bytes accessed | tf_op | source)
XLA Modules:
  0.0 137.4 jit_solution(17894479477822542928)
XLA Ops:
  0.6 0.0 copy-start.7
  0.6 1.0 copy.23
  1.7 0.0 copy-start.4
  1.7 1.1 copy-done.4
  2.8 0.0 copy-start.6
  2.8 0.3 mask_rows.1.b_in
  3.1 0.0 copy-done.7
  3.2 0.1 copy.22
  3.3 0.2 copy-done.6
  3.5 36.9 %gather.1 = (bf16[16,112,256]{2,1,0:T(8,128)(2,1)S(1)}, bf16[4,112,1792]{2,1,0:T(8,128)(2,1)S(1)}, bf16[4,112,256]{2,1,0:T(8,128)(2,1)S(1)}, f32[4,112,256]{2,1,0:T(8,128)S(1)}) custom-call(bf16[4,112,256]{2,1,0:T(8,128)(2,1)S(1)} %pad.8.x_in, bf16[112,1792]{1,0:T(8,128)(2,1)S(1)} %mask_rows.1.b_in, f32[4,112,256]{2,1,0:T(8,128)S(1)} %pad.9.ct_ref, ...), custom_call_target="tpu_custom_call" | custom-call | tf_op jit(solution)/shard_map/gather/pallas_call | solution.py:357
  40.4 0.0 copy-start
  40.4 1.2 copy-done
  41.6 0.0 copy-start.2
  41.6 0.9 copy-done.2
  42.5 0.0 copy-start.5
  42.5 0.7 copy-done.5
  43.2 29.5 %attention.1 = (bf16[1792,256]{1,0:T(8,128)(2,1)}, f32[8,256,128]{2,1,0:T(8,128)}) custom-call(bf16[1792,256]{1,0:T(8,128)(2,1)} %bitcast.33, bf16[448,256]{1,0:T(8,128)(2,1)} %bitcast.36, bf16[448,1792]{1,0:T(8,128)(2,1)} %bitcast.31, bf16[256,256]{1,0:T(8,128)(2,1)} %wq_ref.1, bf16[256,256]{1,0:T(8,128)(2,1)} %wk_ref.1, bf16[256,256]{1,0:T(8,128)(2,1)} %wv_ref.1, ...), custom_call_target="tpu_custom_call" | custom-call | tf_op jit(solution)/shard_map/attention/pallas_call | solution.py:381
  72.7 0.0 copy-start.1
  72.7 1.2 copy-done.1
  74.0 0.0 copy-start.3
  74.0 1.2 copy-done.3
  75.1 59.8 %scatter.1 = (bf16[16,112,256]{2,1,0:T(8,128)(2,1)S(1)}, bf16[16,128,128]{2,1,0:T(8,128)(2,1)S(1)}) custom-call(bf16[16,112,256]{2,1,0:T(8,128)(2,1)S(1)} %bitcast.34, f32[16,128,128]{2,1,0:T(8,128)S(1)} %bitcast.32), custom_call_target="tpu_custom_call" | custom-call | tf_op jit(solution)/shard_map/scatter/pallas_call | solution.py:416
  135.0 0.1 fusion.8
  135.1 0.1 fusion
  135.2 1.0 copy.17
  136.2 0.1 convert.1
  136.3 0.1 slice_bitcast_fusion
  136.4 1.0 fusion.7
  (2 shorter events, 0.1 us)
Async XLA Ops:
  0.6 2.5 %copy-start.7 = (f32[105,4,256]{2,1,0:T(4,128)S(1)}, f32[105,4,256]{2,1,0:T(4,128)}, u32[]{:S(2)}) copy-start(f32[105,4,256]{2,1,0:T(4,128)} %param.15) | copy-start | bytes 1290244
  1.7 1.1 copy-start.4
  2.8 0.7 copy-start.6
  40.4 1.2 copy-start
  41.6 0.9 copy-start.2
  42.5 0.7 copy-start.5
  72.7 1.2 copy-start.1
  74.0 1.2 copy-start.3

commit v3 on v2

--- a/solution.py
+++ b/solution.py
@@ -12,6 +12,8 @@
 NS = 16
 NT = 16
 NY = 4
+NJ = 8
+NZ = 8
 MESH = pl.DeviceIdType.MESH
 BF = jnp.bfloat16
 F32 = jnp.float32
@@ -156,42 +158,47 @@
 SPREAD = (8, 4, 12, 5, 13, 7, 11, 6, 14, 9, 10, 3, 1, 2, 15)
 
 
-def greet(axes):
+def greet(diagonal):
+    me = lax.axis_index("space")
+    t = lax.axis_index("tm")
+    j = lax.rem(t, NJ)
+    peers = [{"space": lax.rem(me + k, NS)} for k in range(1, NS)]
+    peers += [{"tm": t - j + lax.rem(j + k, NJ)} for k in range(1, NJ)]
+    across = lax.rem(t + NJ, NT)
+    peers.append({"tm": across})
+    if diagonal:
+        peers += [{"tm": across, "space": lax.rem(me + NY * k, NS)} for k in range(1, NS // NY)]
     barrier = pltpu.get_barrier_semaphore()
-    count = 0
-    for axis, extent in axes:
-        me = lax.axis_index(axis)
-        for k in range(1, extent):
-            pl.semaphore_signal(
-                barrier, inc=1, device_id={axis: lax.rem(me + k, extent)}, device_id_type=MESH
-            )
-            count += 1
-    pl.semaphore_wait(barrier, count)
-
-
-def push(src, dst, sems, i, axis, to):
+    for peer in peers:
+        pl.semaphore_signal(barrier, inc=1, device_id=peer, device_id_type=MESH)
+    pl.semaphore_wait(barrier, len(peers))
+
+
+def push(src, dst, sems, i, **to):
     return pltpu.make_async_remote_copy(
         src_ref=src,
         dst_ref=dst,
         send_sem=sems[0].at[i],
         recv_sem=sems[1].at[i],
-        device_id={axis: to},
+        device_id=to,
         device_id_type=MESH,
     )
 
 
 def gather_kernel(
     x_in, b_in, ct_ref, decay_ref, x_out, b_out, gb_out, grads_ref,
-    m_send, d_send, m_got, d_got, gb_send, carried,
+    got, late, late_in, gb_send, carried, run, prod, before,
     s0, r0, s1, r1, s2, r2, s3, r3, s4, r4, s5, r5, own,
 ):
-    rounds = ct_ref.shape[0]
+    rounds, pad, _ = ct_ref.shape
     cols = b_in.shape[1] // 2
     me = lax.axis_index("space")
     y = lax.rem(me, NY)
     base = me - y
     t = lax.axis_index("tm")
     core = lax.rem(t, 2)
+    j = lax.rem(t, NJ)
+    upper = t >= NJ
     half = pl.ds(pl.multiple_of(core * cols, cols), cols)
 
     level = ct_ref[rounds - 1]
@@ -199,42 +206,56 @@
     for r in range(rounds - 2, -1, -1):
         level = ct_ref[r] + decay_ref[r + 1 : r + 2, :] * level
         reach = reach * decay_ref[r : r + 1, :]
-    m_send[...] = (decay_ref[0:1, :] * level).astype(BF)
-    d_send[...] = jnp.broadcast_to(reach, d_send.shape)
-
-    greet((("tm", NT), ("space", NS)))
-    for k in range(1, NT):
-        to = jnp.maximum(t - k, 0)
-        pl.when(t >= k)(push(m_send, m_got.at[k - 1], (s3, r3), k, "tm", to).start)
-        pl.when(t >= k)(push(d_send, d_got.at[k - 1], (s4, r4), k, "tm", to).start)
+    got[j, 0:pad, :] = (decay_ref[0:1, :] * level).astype(BF)
+    d0 = reach.astype(BF).astype(F32)
+    d1 = (reach - d0).astype(BF).astype(F32)
+    d2 = reach - d0 - d1
+    row = lax.broadcasted_iota(jnp.int32, (16, reach.shape[1]), 0)
+    got[j, pad : pad + 16, :] = jnp.where(row == 0, d0, jnp.where(row == 1, d1, d2)).astype(BF)
+
+    greet(False)
+    scan = []
+    for k in range(1, NJ):
+        to = t - j + lax.rem(j + k, NJ)
+        scan.append(push(got.at[j], got.at[j], (s3, r3), k, tm=to))
     tokens = []
     for k in SPREAD:
         to = lax.rem(me + k, NS)
-        tokens.append(push(x_in.at[lax.rem(to, NY)], x_out.at[me], (s0, r0), k, "space", to))
+        tokens.append(push(x_in.at[lax.rem(to, NY)], x_out.at[me], (s0, r0), k, space=to))
     masks = []
     for k in range(1, NY):
-        to = lax.rem(y + k, NY)
-        masks.append(
-            push(b_in.at[:, half], b_out.at[y, :, half], (s2, r2), k, "space", base + to)
-        )
+        to = base + lax.rem(y + k, NY)
+        masks.append(push(b_in.at[:, half], b_out.at[y, :, half], (s2, r2), k, space=to))
     local = [
         pltpu.make_async_copy(x_in.at[y], x_out.at[me], own.at[0]),
         pltpu.make_async_copy(b_in, b_out.at[y], own.at[1]),
     ]
-    for copy in masks + tokens + local:
-        copy.start()
-
-    for k in range(1, NT):
-        to = jnp.maximum(t - k, 0)
-        for src, dst, sems in ((m_send, m_got, (s3, r3)), (d_send, d_got, (s4, r4))):
-            copy = push(src, dst.at[k - 1], sems, k, "tm", to)
-            pl.when(t + k < NT)(copy.wait_recv)
-    carried[...] = jnp.zeros(carried.shape, F32)
-    for k in range(NT - 1, 0, -1):
-
-        @pl.when(t + k < NT)
+    for copy in scan + masks + tokens + local:
+        copy.start()
+
+    for copy in scan:
+        copy.wait()
+    run[...] = jnp.zeros(run.shape, F32)
+    prod[...] = jnp.ones(prod.shape, F32)
+    for i in range(NJ - 1, -1, -1):
+
+        @pl.when(j == i)
         def _():
-            carried[...] = m_got[k - 1].astype(F32) + d_got[k - 1, 0:1, :] * carried[...]
+            carried[...] = run[...]
+            before[...] = prod[...]
+
+        tail = got[i, pad : pad + 16, :].astype(F32)
+        step = tail[0:1] + tail[1:2] + tail[2:3]
+        run[...] = got[i, 0:pad, :].astype(F32) + step * run[...]
+        prod[...] = step * prod[...]
+    late[...] = run[...].astype(BF)
+    over = push(late, late_in, (s4, r4), 0, tm=lax.rem(t + NJ, NT))
+    pl.when(upper)(over.start)
+
+    @pl.when(jnp.logical_not(upper))
+    def _():
+        over.wait_recv()
+        carried[...] += before[0:1, :] * late_in[...].astype(F32)
 
     level = ct_ref[rounds - 1] + carried[...]
     for r in range(rounds - 1, -1, -1):
@@ -245,7 +266,7 @@
     ups = []
     for k in range(1, NY):
         to = lax.rem(y + k, NY)
-        ups.append(push(gb_send.at[to], gb_out.at[y], (s1, r1), k, "space", base + to))
+        ups.append(push(gb_send.at[to], gb_out.at[y], (s1, r1), k, space=base + to))
     ups.append(pltpu.make_async_copy(gb_send.at[y], gb_out.at[y], own.at[2]))
     for copy in ups:
         copy.start()
@@ -253,80 +274,96 @@
     shared = []
     for k in range(1, NY):
         masks[k - 1].wait()
-        src = lax.rem(y - k + NY, NY)
-        copy = push(
-            b_out.at[src, :, half], b_out.at[src, :, half], (s5, r5), k, "tm", t + 1 - 2 * core
-        )
+        piece = b_out.at[lax.rem(y - k + NY, NY), :, half]
+        copy = push(piece, piece, (s5, r5), k, tm=t + 1 - 2 * core)
         copy.start()
         shared.append(copy)
-    for k in range(1, NT):
-        to = jnp.maximum(t - k, 0)
-        for src, dst, sems in ((m_send, m_got, (s3, r3)), (d_send, d_got, (s4, r4))):
-            pl.when(t >= k)(push(src, dst.at[k - 1], sems, k, "tm", to).wait_send)
+    pl.when(upper)(over.wait_send)
     for copy in tokens + local + ups + shared:
         copy.wait()
 
 
 def scatter_kernel(
-    c_in, g_in, c_out, g_out, send1, got1, part, got2, mine, whole, send4,
-    s0, r0, s1, r1, s2, r2, s3, r3, s4, r4, own,
+    c_in, g_in, c_out, g_out, send1, got1, part, got2, send3, got3, got4,
+    s0, r0, s1, r1, s2, r2, s3, r3, s4, r4, s5, r5, own,
 ):
     me = lax.axis_index("space")
     t = lax.axis_index("tm")
-    for i in range(NT):
+    y = lax.rem(me, NY)
+    base = me - y
+    j = lax.rem(t, NJ)
+    line = lax.div(me, NY) * 2 + lax.div(t, NJ)
+    for i in range(NJ):
         send1[i] = g_in[i].astype(send1.dtype)
-    greet((("tm", NT), ("space", NS)))
+    greet(True)
 
     first = []
-    for k in range(1, NT):
-        to = lax.rem(t + k, NT)
-        first.append(push(send1.at[to], got1.at[t], (s0, r0), k, "tm", to))
+    for k in range(1, NJ):
+        to = lax.rem(j + k, NJ)
+        first.append(push(send1.at[to], got1.at[j], (s0, r0), k, tm=t - j + to))
     tokens = []
     for k in SPREAD:
         to = lax.rem(me + k, NS)
-        tokens.append(push(c_in.at[to], c_out.at[me], (s4, r4), k, "space", to))
+        tokens.append(push(c_in.at[to], c_out.at[me], (s4, r4), k, space=to))
     tokens.append(pltpu.make_async_copy(c_in.at[me], c_out.at[me], own))
     for copy in first + tokens:
         copy.start()
-    total = g_in[t]
+    total = g_in[j]
     for copy in first:
         copy.wait()
-    for k in range(1, NT):
-        total = total + got1[lax.rem(t + k, NT)].astype(F32)
+    for k in range(1, NJ):
+        total = total + got1[lax.rem(j + k, NJ)].astype(F32)
     part[...] = total.reshape(part.shape)
 
     second = []
-    for k in range(1, NS):
-        to = lax.rem(me + k, NS)
-        second.append(push(part.at[to], got2.at[me], (s1, r1), k, "space", to))
+    for k in range(1, NY):
+        to = lax.rem(y + k, NY)
+        second.append(push(part.at[to], got2.at[y], (s1, r1), k, space=base + to))
     for copy in second:
         copy.start()
-    total = part[me]
+    total = part[y]
     for copy in second:
         copy.wait()
-    for k in range(1, NS):
-        total = total + got2[lax.rem(me + k, NS)]
-    mine[...] = total
-    whole[me] = total
+    for k in range(1, NY):
+        total = total + got2[lax.rem(y + k, NY)]
+    send3[...] = total.astype(send3.dtype)
+    got3[line] = send3[...]
 
     third = []
-    for k in range(1, NS):
-        to = lax.rem(me + k, NS)
-        third.append(push(mine, whole.at[me], (s2, r2), k, "space", to))
+    for k in range(1, NZ):
+        to = lax.rem(line + k, NZ)
+        third.append(
+            push(
+                send3, got3.at[line], (s2, r2), k,
+                tm=lax.rem(to, 2) * NJ + j, space=lax.div(to, 2) * NY + y,
+            )
+        )
     for copy in third:
         copy.start()
     for copy in third:
         copy.wait()
-    send4[...] = whole[...].reshape(send4.shape).astype(send4.dtype)
-    g_out[t] = send4[...]
+    total = got3[0].astype(F32)
+    for i in range(1, NZ):
+        total = total + got3[i].astype(F32)
+    got4[y] = total.astype(got4.dtype)
 
     fourth = []
-    for k in range(1, NT):
-        to = lax.rem(t + k, NT)
-        fourth.append(push(send4, g_out.at[t], (s3, r3), k, "tm", to))
+    for k in range(1, NY):
+        to = base + lax.rem(y + k, NY)
+        fourth.append(push(got4.at[y], got4.at[y], (s3, r3), k, space=to))
     for copy in fourth:
         copy.start()
-    for copy in fourth + tokens:
+    for copy in fourth:
+        copy.wait()
+    g_out[j] = got4[...].reshape(g_out.shape[1:])
+
+    fifth = []
+    for k in range(1, NJ):
+        to = t - j + lax.rem(j + k, NJ)
+        fifth.append(push(g_out.at[j], g_out.at[j], (s5, r5), k, tm=to))
+    for copy in fifth:
+        copy.start()
+    for copy in fifth + tokens:
         copy.wait()
 
 
@@ -365,14 +402,16 @@
         in_specs=[ANY, ANY, VM, VM],
         out_specs=[ANY, ANY, ANY, VM],
         scratch_shapes=[
+            pltpu.VMEM((NJ, pad + 16, width), BF),
             pltpu.VMEM((pad, width), BF),
-            pltpu.VMEM((8, width), F32),
-            pltpu.VMEM((NT - 1, pad, width), BF),
-            pltpu.VMEM((NT - 1, 8, width), F32),
+            pltpu.VMEM((pad, width), BF),
             pltpu.VMEM((rounds, pad, width), BF),
             pltpu.VMEM((pad, width), F32),
+            pltpu.VMEM((pad, width), F32),
+            pltpu.VMEM((8, width), F32),
+            pltpu.VMEM((8, width), F32),
             dma(NS), dma(NS), dma(NY), dma(NY), dma(NY), dma(NY),
-            dma(NT), dma(NT), dma(NT), dma(NT), dma(NY), dma(NY), dma(3),
+            dma(NJ), dma(NJ), dma(1), dma(1), dma(NY), dma(NY), dma(3),
         ],
         compiler_params=params(cid=1),
         name="gather",
@@ -415,23 +454,23 @@
     wire = BF
     parts, g = pl.pallas_call(
         scatter_kernel,
-        out_shape=(sds((NS, pad, width), BF), sds((NT, 128, 128), wire)),
+        out_shape=(sds((NS, pad, width), BF), sds((NJ, 256, 128), wire)),
         in_specs=[ANY, VM],
         out_specs=[ANY, VM],
         scratch_shapes=[
-            pltpu.VMEM((NT, 128, 128), wire),
-            pltpu.VMEM((NT, 128, 128), wire),
-            pltpu.VMEM((NS, 8, 128), F32),
-            pltpu.VMEM((NS, 8, 128), F32),
-            pltpu.VMEM((8, 128), F32),
-            pltpu.VMEM((NS, 8, 128), F32),
-            pltpu.VMEM((128, 128), wire),
-            dma(NT), dma(NT), dma(NS), dma(NS), dma(NS), dma(NS), dma(NT), dma(NT),
-            dma(NS), dma(NS), pltpu.SemaphoreType.DMA,
+            pltpu.VMEM((NJ, 256, 128), wire),
+            pltpu.VMEM((NJ, 256, 128), wire),
+            pltpu.VMEM((NY, 64, 128), F32),
+            pltpu.VMEM((NY, 64, 128), F32),
+            pltpu.VMEM((64, 128), wire),
+            pltpu.VMEM((NZ, 64, 128), wire),
+            pltpu.VMEM((NY, 64, 128), wire),
+            dma(NJ), dma(NJ), dma(NY), dma(NY), dma(NZ), dma(NZ), dma(NY), dma(NY),
+            dma(NS), dma(NS), dma(NJ), dma(NJ), pltpu.SemaphoreType.DMA,
         ],
         compiler_params=params(cid=2),
         name="scatter",
-    )(c.reshape(NS, pad, width), g.reshape(NT, 128, 128))
+    )(c.reshape(NS, pad, width), g)
     parts = parts.reshape(NS // NY, rounds, pad, width)
     gt = grads + sum(parts[z].astype(F32) for z in range(NS // NY))
     g = g.astype(F32).reshape(4, 2, width, 128)

time: 138 us -> 121 us (0.88)
  Pallas kernels: 127 us -> 110 us
    pallas_call x1, Pallas kernels: 59.8 us -> 43.2 us  [shards(): pl.pallas_call(scatter_kernel, out_shape=(sds((NS, pad, width), BF), sds(...]
where the time goes in v3:
time: 121 us
  Pallas kernels  110 us (91%)
  local copies, waits for them, and re-layouts  8.86 us (7%)
    pallas_call x1, Pallas kernels, shards(): pl.pallas_call(scatter_kernel, out_shape=(sds((NS, pad, width), BF), sds(...  43.2 us
    pallas_call x1, Pallas kernels, shards(): pl.pallas_call(gather_kernel, out_shape=(sds((NS, pad, width), BF), sds((...  36.8 us
    pallas_call x1, Pallas kernels, shards(): pl.pallas_call(functools.partial(attention_kernel, scale), out_shape=(sds...  29.5 us
    unnamed x19, local copies, waits for them, and re-layouts  8.68 us

profile of v3, /device:TPU:1, one launch (start us, length us, event | category | flops | bytes accessed | tf_op | source)
XLA Modules:
  0.0 120.6 jit_solution(11363973237823655949)
XLA Ops:
  0.6 0.0 copy-start.7
  0.6 1.0 copy.23
  1.7 0.0 copy-start.4
  1.7 1.1 copy-done.4
  2.8 0.0 copy-start.6
  2.8 0.3 mask_rows.1.b_in
  3.1 0.0 copy-done.7
  3.2 0.1 copy.22
  3.3 0.2 copy-done.6
  3.5 36.8 %gather.1 = (bf16[16,112,256]{2,1,0:T(8,128)(2,1)S(1)}, bf16[4,112,1792]{2,1,0:T(8,128)(2,1)S(1)}, bf16[4,112,256]{2,1,0:T(8,128)(2,1)S(1)}, f32[4,112,256]{2,1,0:T(8,128)S(1)}) custom-call(bf16[4,112,256]{2,1,0:T(8,128)(2,1)S(1)} %pad.8.x_in, bf16[112,1792]{1,0:T(8,128)(2,1)S(1)} %mask_rows.1.b_in, f32[4,112,256]{2,1,0:T(8,128)S(1)} %pad.9.ct_ref, ...), custom_call_target="tpu_custom_call" | custom-call | tf_op jit(solution)/shard_map/gather/pallas_call | solution.py:394
  40.3 0.0 copy-start
  40.3 1.2 copy-done
  41.5 0.0 copy-start.2
  41.5 0.9 copy-done.2
  42.4 0.0 copy-start.5
  42.4 0.7 copy-done.5
  43.1 29.5 %attention.1 = (bf16[1792,256]{1,0:T(8,128)(2,1)}, f32[8,256,128]{2,1,0:T(8,128)}) custom-call(bf16[1792,256]{1,0:T(8,128)(2,1)} %bitcast.31, bf16[448,256]{1,0:T(8,128)(2,1)} %bitcast.34, bf16[448,1792]{1,0:T(8,128)(2,1)} %bitcast.30, bf16[256,256]{1,0:T(8,128)(2,1)} %wq_ref.1, bf16[256,256]{1,0:T(8,128)(2,1)} %wk_ref.1, bf16[256,256]{1,0:T(8,128)(2,1)} %wv_ref.1, ...), custom_call_target="tpu_custom_call" | custom-call | tf_op jit(solution)/shard_map/attention/pallas_call | solution.py:420
  72.6 0.0 copy-start.1
  72.6 1.2 %copy-done.1 = f32[8,256,128]{2,1,0:T(8,128)S(1)} copy-done((f32[8,256,128]{2,1,0:T(8,128)S(1)}, f32[8,256,128]{2,1,0:T(8,128)}, u32[]{:S(2)}) %copy-start.1) | copy-done | bytes 1048600
  73.9 0.0 copy-start.3
  73.9 1.2 copy-done.3
  75.0 43.2 %scatter.1 = (bf16[16,112,256]{2,1,0:T(8,128)(2,1)S(1)}, bf16[8,256,128]{2,1,0:T(8,128)(2,1)S(1)}) custom-call(bf16[16,112,256]{2,1,0:T(8,128)(2,1)S(1)} %bitcast.32, f32[8,256,128]{2,1,0:T(8,128)S(1)} %copy-done.1), custom_call_target="tpu_custom_call" | custom-call | tf_op jit(solution)/shard_map/scatter/pallas_call | solution.py:455
  118.2 0.1 fusion.8
  118.3 0.1 fusion
  118.4 1.0 copy.17
  119.5 0.1 convert.1
  119.5 0.1 slice_bitcast_fusion
  119.6 1.0 fusion.7
  (2 shorter events, 0.1 us)
Async XLA Ops:
  0.6 2.5 %copy-start.7 = (f32[105,4,256]{2,1,0:T(4,128)S(1)}, f32[105,4,256]{2,1,0:T(4,128)}, u32[]{:S(2)}) copy-start(f32[105,4,256]{2,1,0:T(4,128)} %param.15) | copy-start | bytes 1290244
  1.7 1.1 copy-start.4
  2.8 0.7 copy-start.6
  40.3 1.2 copy-start
  41.5 0.9 copy-start.2
  42.4 0.7 copy-start.5
  72.6 1.2 %copy-start.1 = (f32[8,256,128]{2,1,0:T(8,128)S(1)}, f32[8,256,128]{2,1,0:T(8,128)}, u32[]{:S(2)}) copy-start(f32[8,256,128]{2,1,0:T(8,128)} %get-tuple-element.18.g_in) | copy-start | bytes 3145732
  73.9 1.2 copy-start.3

commit v4 on v3

--- a/solution.py
+++ b/solution.py
@@ -24,7 +24,7 @@
 ANY = pl.BlockSpec(memory_space=pl.ANY)
 
 
-def params(mib=48, cid=None):
+def params(mib=16, cid=None):
     if cid is None:
         return pltpu.CompilerParams(vmem_limit_bytes=mib * MIB)
     return pltpu.CompilerParams(
@@ -155,7 +155,7 @@
         g_ref[2 * i + 1] = g[:, half:width]
 
 
-SPREAD = (8, 4, 12, 5, 13, 7, 11, 6, 14, 9, 10, 3, 1, 2, 15)
+SPREAD = (8, 4, 12, 5, 11, 9, 1, 13, 7, 6, 10, 14, 3, 2, 15)
 
 
 def greet(diagonal):
@@ -171,7 +171,7 @@
     barrier = pltpu.get_barrier_semaphore()
     for peer in peers:
         pl.semaphore_signal(barrier, inc=1, device_id=peer, device_id_type=MESH)
-    pl.semaphore_wait(barrier, len(peers))
+    return lambda: pl.semaphore_wait(barrier, len(peers))
 
 
 def push(src, dst, sems, i, **to):
@@ -200,6 +200,7 @@
     j = lax.rem(t, NJ)
     upper = t >= NJ
     half = pl.ds(pl.multiple_of(core * cols, cols), cols)
+    all_here = greet(False)
 
     level = ct_ref[rounds - 1]
     reach = decay_ref[rounds - 1 : rounds, :]
@@ -213,7 +214,7 @@
     row = lax.broadcasted_iota(jnp.int32, (16, reach.shape[1]), 0)
     got[j, pad : pad + 16, :] = jnp.where(row == 0, d0, jnp.where(row == 1, d1, d2)).astype(BF)
 
-    greet(False)
+    all_here()
     scan = []
     for k in range(1, NJ):
         to = t - j + lax.rem(j + k, NJ)
@@ -293,9 +294,10 @@
     base = me - y
     j = lax.rem(t, NJ)
     line = lax.div(me, NY) * 2 + lax.div(t, NJ)
+    all_here = greet(True)
     for i in range(NJ):
         send1[i] = g_in[i].astype(send1.dtype)
-    greet(True)
+    all_here()
 
     first = []
     for k in range(1, NJ):
@@ -306,7 +308,8 @@
         to = lax.rem(me + k, NS)
         tokens.append(push(c_in.at[to], c_out.at[me], (s4, r4), k, space=to))
     tokens.append(pltpu.make_async_copy(c_in.at[me], c_out.at[me], own))
-    for copy in first + tokens:
+    early, later = tokens[:7] + tokens[-1:], tokens[7:-1]
+    for copy in first + early:
         copy.start()
     total = g_in[j]
     for copy in first:
@@ -338,7 +341,7 @@
                 tm=lax.rem(to, 2) * NJ + j, space=lax.div(to, 2) * NY + y,
             )
         )
-    for copy in third:
+    for copy in third + later:
         copy.start()
     for copy in third:
         copy.wait()
@@ -442,7 +445,7 @@
             pltpu.VMEM((width, keys), F32),
             pltpu.VMEM((width, keys), F32),
         ],
-        compiler_params=params(58),
+        compiler_params=params(42),
         name="attention",
     )(
         x_all.reshape(keys, width),

time: 121 us -> 113 us (0.934)
  local copies, waits for them, and re-layouts: 8.86 us -> 3.66 us
  Pallas kernels: 110 us -> 107 us
    unnamed x19 -> x17, local copies, waits for them, and re-layouts: 8.68 us -> 3.47 us
    pallas_call x1, Pallas kernels: 29.5 us -> 26.6 us  [shards(): pl.pallas_call(functools.partial(attention_kernel, scale), out_shape=(sds...]
where the time goes in v4:
time: 113 us; the launch traced here: 112 us
  Pallas kernels  107 us (95%)
  local copies, waits for them, and re-layouts  3.66 us (3%)
  other arithmetic  1.18 us (1%)
    pallas_call x1, Pallas kernels, shards(): pl.pallas_call(scatter_kernel, out_shape=(sds((NS, pad, width), BF), sds(...  43.1 us
    pallas_call x1, Pallas kernels, shards(): pl.pallas_call(gather_kernel, out_shape=(sds((NS, pad, width), BF), sds((...  36.8 us
    pallas_call x1, Pallas kernels, shards(): pl.pallas_call(functools.partial(attention_kernel, scale), out_shape=(sds...  26.6 us
    unnamed x17, local copies, waits for them, and re-layouts  3.47 us

profile of v4, /device:TPU:1, one launch (start us, length us, event | category | flops | bytes accessed | tf_op | source)
XLA Modules:
  0.0 112.4 jit_solution(3143522657668711675)
XLA Ops:
  0.6 0.0 copy-start.6
  0.6 1.0 copy.23
  1.7 0.0 copy-start
  1.7 1.1 %copy-done = s32[105,1680]{1,0:T(8,128)S(1)} copy-done((s32[105,1680]{1,0:T(8,128)S(1)}, s32[105,1680]{1,0:T(8,128)}, u32[]{:S(2)}) %copy-start) | copy-done | bytes 705624
  2.8 0.0 copy-start.5
  2.8 0.3 mask_rows.1.b_in
  3.1 0.0 copy-done.6
  3.2 0.0 copy-start.1
  3.2 0.0 copy-start.2
  3.2 0.0 copy-start.3
  3.2 0.0 copy-start.4
  3.2 0.1 copy.22
  3.3 0.2 copy-done.5
  3.5 36.8 %gather.1 = (bf16[16,112,256]{2,1,0:T(8,128)(2,1)S(1)}, bf16[4,112,1792]{2,1,0:T(8,128)(2,1)S(1)}, bf16[4,112,256]{2,1,0:T(8,128)(2,1)S(1)}, f32[4,112,256]{2,1,0:T(8,128)S(1)}) custom-call(bf16[4,112,256]{2,1,0:T(8,128)(2,1)S(1)} %pad.8.x_in, bf16[112,1792]{1,0:T(8,128)(2,1)S(1)} %mask_rows.1.b_in, f32[4,112,256]{2,1,0:T(8,128)S(1)} %pad.9.ct_ref, ...), custom_call_target="tpu_custom_call" | custom-call | tf_op jit(solution)/shard_map/gather/pallas_call | solution.py:397
  40.3 0.0 copy-done.1
  40.3 0.0 copy-done.2
  40.3 0.0 copy-done.3
  40.3 0.0 copy-done.4
  40.3 26.6 %attention.1 = (bf16[1792,256]{1,0:T(8,128)(2,1)S(1)}, f32[8,256,128]{2,1,0:T(8,128)S(1)}) custom-call(bf16[1792,256]{1,0:T(8,128)(2,1)S(1)} %bitcast.31, bf16[448,256]{1,0:T(8,128)(2,1)S(1)} %bitcast.34, bf16[448,1792]{1,0:T(8,128)(2,1)S(1)} %bitcast.30, bf16[256,256]{1,0:T(8,128)(2,1)S(1)} %copy-done.1, bf16[256,256]{1,0:T(8,128)(2,1)S(1)} %copy-done.2, ...), custom_call_target="tpu_custom_call" | custom-call | tf_op jit(solution)/shard_map/attention/pallas_call | solution.py:423
  66.9 43.1 %scatter.1 = (bf16[16,112,256]{2,1,0:T(8,128)(2,1)S(1)}, bf16[8,256,128]{2,1,0:T(8,128)(2,1)S(1)}) custom-call(bf16[16,112,256]{2,1,0:T(8,128)(2,1)S(1)} %bitcast.32, f32[8,256,128]{2,1,0:T(8,128)S(1)} %get-tuple-element.18.g_in), custom_call_target="tpu_custom_call" | custom-call | tf_op jit(solution)/shard_map/scatter/pallas_call | solution.py:458
  110.0 0.1 fusion.8
  110.1 0.1 fusion
  110.2 1.0 copy.17
  111.2 0.1 convert.1
  111.3 0.1 slice_bitcast_fusion
  111.4 1.0 fusion.7
  (2 shorter events, 0.1 us)
Async XLA Ops:
  0.6 2.5 %copy-start.6 = (f32[105,4,256]{2,1,0:T(4,128)S(1)}, f32[105,4,256]{2,1,0:T(4,128)}, u32[]{:S(2)}) copy-start(f32[105,4,256]{2,1,0:T(4,128)} %param.15) | copy-start | bytes 1290244
  1.7 1.1 %copy-start = (s32[105,1680]{1,0:T(8,128)S(1)}, s32[105,1680]{1,0:T(8,128)}, u32[]{:S(2)}) copy-start(s32[105,1680]{1,0:T(8,128)} %mask_ref.1) | copy-start | bytes 2116804
  2.8 0.7 copy-start.5
  3.2 37.1 %copy-start.1 = (bf16[256,256]{1,0:T(8,128)(2,1)S(1)}, bf16[256,256]{1,0:T(8,128)(2,1)}, u32[]{:S(2)}) copy-start(bf16[256,256]{1,0:T(8,128)(2,1)} %wq_ref.1) | copy-start | bytes 393220
  3.2 37.1 %copy-start.2 = (bf16[256,256]{1,0:T(8,128)(2,1)S(1)}, bf16[256,256]{1,0:T(8,128)(2,1)}, u32[]{:S(2)}) copy-start(bf16[256,256]{1,0:T(8,128)(2,1)} %wk_ref.1) | copy-start | bytes 393220
  3.2 37.1 %copy-start.3 = (bf16[256,256]{1,0:T(8,128)(2,1)S(1)}, bf16[256,256]{1,0:T(8,128)(2,1)}, u32[]{:S(2)}) copy-start(bf16[256,256]{1,0:T(8,128)(2,1)} %wv_ref.1) | copy-start | bytes 393220
  3.2 37.1 %copy-start.4 = (bf16[256,256]{1,0:T(8,128)(2,1)S(1)}, bf16[256,256]{1,0:T(8,128)(2,1)}, u32[]{:S(2)}) copy-start(bf16[256,256]{1,0:T(8,128)(2,1)} %wo_ref.1) | copy-start | bytes 393220

commit v5 on v4

--- a/solution.py
+++ b/solution.py
@@ -155,19 +155,19 @@
         g_ref[2 * i + 1] = g[:, half:width]
 
 
-SPREAD = (8, 4, 12, 5, 11, 9, 1, 13, 7, 6, 10, 14, 3, 2, 15)
-
-
 def greet(diagonal):
     me = lax.axis_index("space")
     t = lax.axis_index("tm")
+    y = lax.rem(me, NY)
     j = lax.rem(t, NJ)
-    peers = [{"space": lax.rem(me + k, NS)} for k in range(1, NS)]
+    across = lax.rem(t + NJ, NT)
+    far = range(1, NS // NY)
+    peers = [{"space": me - y + lax.rem(y + k, NY)} for k in range(1, NY)]
+    peers += [{"space": lax.rem(me + NY * k, NS)} for k in far]
     peers += [{"tm": t - j + lax.rem(j + k, NJ)} for k in range(1, NJ)]
-    across = lax.rem(t + NJ, NT)
     peers.append({"tm": across})
     if diagonal:
-        peers += [{"tm": across, "space": lax.rem(me + NY * k, NS)} for k in range(1, NS // NY)]
+        peers += [{"tm": across, "space": lax.rem(me + NY * k, NS)} for k in far]
     barrier = pltpu.get_barrier_semaphore()
     for peer in peers:
         pl.semaphore_signal(barrier, inc=1, device_id=peer, device_id_type=MESH)
@@ -188,13 +188,16 @@
 def gather_kernel(
     x_in, b_in, ct_ref, decay_ref, x_out, b_out, gb_out, grads_ref,
     got, late, late_in, gb_send, carried, run, prod, before,
-    s0, r0, s1, r1, s2, r2, s3, r3, s4, r4, s5, r5, own,
+    s0, r0, s1, r1, s2, r2, s3, r3, s4, r4, s5, r5, s6, r6, s7, r7, s8, r8, s9, r9, own,
 ):
     rounds, pad, _ = ct_ref.shape
     cols = b_in.shape[1] // 2
     me = lax.axis_index("space")
     y = lax.rem(me, NY)
     base = me - y
+    depth = NS // NY
+    z = lax.div(me, NY)
+    right, left = lax.rem(z + 1, depth), lax.rem(z + depth - 1, depth)
     t = lax.axis_index("tm")
     core = lax.rem(t, 2)
     j = lax.rem(t, NJ)
@@ -220,9 +223,24 @@
         to = t - j + lax.rem(j + k, NJ)
         scan.append(push(got.at[j], got.at[j], (s3, r3), k, tm=to))
     tokens = []
-    for k in SPREAD:
-        to = lax.rem(me + k, NS)
-        tokens.append(push(x_in.at[lax.rem(to, NY)], x_out.at[me], (s0, r0), k, space=to))
+    for k in range(1, NY):
+        to = lax.rem(y + k, NY)
+        tokens.append(push(x_in.at[to], x_out.at[me], (s0, r0), k, space=base + to))
+    sides = []
+    for k in range(NY):
+        slot = base + lax.rem(y - k + NY, NY)
+        src = x_in.at[y] if k == 0 else x_out.at[slot]
+        sides.append(
+            (
+                push(src, x_out.at[slot], (s6, r6), k, space=right * NY + y),
+                push(src, x_out.at[slot], (s7, r7), k, space=left * NY + y),
+            )
+        )
+    passed = []
+    for k in range(NY):
+        of, to, sems = (left, right, (s8, r8)) if k < 2 else (right, left, (s9, r9))
+        slot = x_out.at[of * NY + lax.rem(y - k + NY, NY)]
+        passed.append(push(slot, slot, sems, k, space=to * NY + y))
     masks = []
     for k in range(1, NY):
         to = base + lax.rem(y + k, NY)
@@ -231,8 +249,12 @@
         pltpu.make_async_copy(x_in.at[y], x_out.at[me], own.at[0]),
         pltpu.make_async_copy(b_in, b_out.at[y], own.at[1]),
     ]
-    for copy in scan + masks + tokens + local:
-        copy.start()
+    for copy in scan + tokens + list(sides[0]) + masks + local:
+        copy.start()
+    for k in range(1, NY):
+        tokens[k - 1].wait()
+        sides[k][0].start()
+        sides[k][1].start()
 
     for copy in scan:
         copy.wait()
@@ -252,6 +274,9 @@
     late[...] = run[...].astype(BF)
     over = push(late, late_in, (s4, r4), 0, tm=lax.rem(t + NJ, NT))
     pl.when(upper)(over.start)
+    for k in range(2):
+        sides[k][0].wait()
+        passed[k].start()
 
     @pl.when(jnp.logical_not(upper))
     def _():
@@ -279,21 +304,29 @@
         copy = push(piece, piece, (s5, r5), k, tm=t + 1 - 2 * core)
         copy.start()
         shared.append(copy)
+    for k in range(2, NY):
+        sides[k][1].wait()
+        passed[k].start()
     pl.when(upper)(over.wait_send)
-    for copy in tokens + local + ups + shared:
+    for copy in (sides[0][1], sides[1][1], sides[2][0], sides[3][0]):
+        copy.wait()
+    for copy in passed + local + ups + shared:
         copy.wait()
 
 
 def scatter_kernel(
     c_in, g_in, c_out, g_out, send1, got1, part, got2, send3, got3, got4,
-    s0, r0, s1, r1, s2, r2, s3, r3, s4, r4, s5, r5, own,
+    far_l, far_r, mix_l, mix_r, got_l, got_r, sum_c, s0, r0, s1, r1, s2, r2, s3, r3, s4, r4, s5, r5, s6, r6,
 ):
     me = lax.axis_index("space")
     t = lax.axis_index("tm")
     y = lax.rem(me, NY)
     base = me - y
     j = lax.rem(t, NJ)
-    line = lax.div(me, NY) * 2 + lax.div(t, NJ)
+    z = lax.div(me, NY)
+    depth = NS // NY
+    right, left, opposite = (lax.rem(z + k, depth) for k in (1, depth - 1, 2))
+    line = z * 2 + lax.div(t, NJ)
     all_here = greet(True)
     for i in range(NJ):
         send1[i] = g_in[i].astype(send1.dtype)
@@ -303,14 +336,35 @@
     for k in range(1, NJ):
         to = lax.rem(j + k, NJ)
         first.append(push(send1.at[to], got1.at[j], (s0, r0), k, tm=t - j + to))
-    tokens = []
-    for k in SPREAD:
-        to = lax.rem(me + k, NS)
-        tokens.append(push(c_in.at[to], c_out.at[me], (s4, r4), k, space=to))
-    tokens.append(pltpu.make_async_copy(c_in.at[me], c_out.at[me], own))
-    early, later = tokens[:7] + tokens[-1:], tokens[7:-1]
-    for copy in first + early:
-        copy.start()
+    two = 2
+    far = [
+        push(c_in.at[pl.ds(opposite * NY, two)], far_l, (s4, r4), 0, space=right * NY + y),
+        push(c_in.at[pl.ds(opposite * NY + two, two)], far_r, (s4, r4), 1, space=left * NY + y),
+    ]
+    near = [
+        push(
+            c_in.at[pl.ds(right * NY + two, two)], got_l.at[pl.ds(two, two)], (s4, r4), 2,
+            space=right * NY + y,
+        ),
+        push(
+            c_in.at[pl.ds(left * NY, two)], got_r.at[pl.ds(0, two)], (s4, r4), 3,
+            space=left * NY + y,
+        ),
+    ]
+    for copy in far + first + near:
+        copy.start()
+    mixed = [
+        push(mix_r, got_l.at[pl.ds(0, two)], (s4, r4), 4, space=right * NY + y),
+        push(mix_l, got_r.at[pl.ds(two, two)], (s4, r4), 5, space=left * NY + y),
+    ]
+    far[0].wait()
+    for i in range(two):
+        mix_r[i] = (c_in[right * NY + i].astype(F32) + far_l[i].astype(F32)).astype(BF)
+    mixed[0].start()
+    far[1].wait()
+    for i in range(two):
+        mix_l[i] = (c_in[left * NY + two + i].astype(F32) + far_r[i].astype(F32)).astype(BF)
+    mixed[1].start()
     total = g_in[j]
     for copy in first:
         copy.wait()
@@ -341,7 +395,7 @@
                 tm=lax.rem(to, 2) * NJ + j, space=lax.div(to, 2) * NY + y,
             )
         )
-    for copy in third + later:
+    for copy in third:
         copy.start()
     for copy in third:
         copy.wait()
@@ -356,6 +410,18 @@
         fourth.append(push(got4.at[y], got4.at[y], (s3, r3), k, space=to))
     for copy in fourth:
         copy.start()
+    for copy in near + mixed:
+        copy.wait()
+    for i in range(NY):
+        block = c_in[z * NY + i].astype(F32) + got_l[i].astype(F32) + got_r[i].astype(F32)
+        sum_c[i] = block.astype(BF)
+    tokens = []
+    for k in range(1, NY):
+        to = lax.rem(y + k, NY)
+        tokens.append(push(sum_c.at[to], c_out.at[y], (s6, r6), k, space=base + to))
+    for copy in tokens:
+        copy.start()
+    c_out[y] = sum_c[y]
     for copy in fourth:
         copy.wait()
     g_out[j] = got4[...].reshape(g_out.shape[1:])
@@ -413,8 +479,9 @@
             pltpu.VMEM((pad, width), F32),
             pltpu.VMEM((8, width), F32),
             pltpu.VMEM((8, width), F32),
-            dma(NS), dma(NS), dma(NY), dma(NY), dma(NY), dma(NY),
-            dma(NJ), dma(NJ), dma(1), dma(1), dma(NY), dma(NY), dma(3),
+            dma(NY), dma(NY), dma(NY), dma(NY), dma(NY), dma(NY),
+            dma(NJ), dma(NJ), dma(1), dma(1), dma(NY), dma(NY),
+            dma(NY), dma(NY), dma(NY), dma(NY), dma(NY), dma(NY), dma(NY), dma(NY), dma(3),
         ],
         compiler_params=params(cid=1),
         name="gather",
@@ -457,9 +524,9 @@
     wire = BF
     parts, g = pl.pallas_call(
         scatter_kernel,
-        out_shape=(sds((NS, pad, width), BF), sds((NJ, 256, 128), wire)),
-        in_specs=[ANY, VM],
-        out_specs=[ANY, VM],
+        out_shape=(sds((rounds, pad, width), BF), sds((NJ, 256, 128), wire)),
+        in_specs=[VM, VM],
+        out_specs=[VM, VM],
         scratch_shapes=[
             pltpu.VMEM((NJ, 256, 128), wire),
             pltpu.VMEM((NJ, 256, 128), wire),
@@ -468,14 +535,20 @@
             pltpu.VMEM((64, 128), wire),
             pltpu.VMEM((NZ, 64, 128), wire),
             pltpu.VMEM((NY, 64, 128), wire),
+            pltpu.VMEM((2, pad, width), BF),
+            pltpu.VMEM((2, pad, width), BF),
+            pltpu.VMEM((2, pad, width), BF),
+            pltpu.VMEM((2, pad, width), BF),
+            pltpu.VMEM((NY, pad, width), BF),
+            pltpu.VMEM((NY, pad, width), BF),
+            pltpu.VMEM((NY, pad, width), BF),
             dma(NJ), dma(NJ), dma(NY), dma(NY), dma(NZ), dma(NZ), dma(NY), dma(NY),
-            dma(NS), dma(NS), dma(NJ), dma(NJ), pltpu.SemaphoreType.DMA,
+            dma(6), dma(6), dma(NJ), dma(NJ), dma(NY), dma(NY),
         ],
         compiler_params=params(cid=2),
         name="scatter",
     )(c.reshape(NS, pad, width), g)
-    parts = parts.reshape(NS // NY, rounds, pad, width)
-    gt = grads + sum(parts[z].astype(F32) for z in range(NS // NY))
+    gt = grads + parts.astype(F32)
     g = g.astype(F32).reshape(4, 2, width, 128)
     g = jnp.concatenate([g[:, 0], g[:, 1]], axis=2)
     grad_tokens = jnp.swapaxes(gt[:, :rows], 0, 1)

time: 113 us -> 99 us (0.88)
  Pallas kernels: 107 us -> 93.4 us
    pallas_call x1, Pallas kernels: 36.8 us -> 28.1 us  [shards(): pl.pallas_call(gather_kernel, out_shape=(sds((NS, pad, width), BF), sds((...]
    pallas_call x1, Pallas kernels: 43.1 us -> 38.4 us  [shards(): pl.pallas_call(scatter_kernel, out_shape=(sds((rounds, pad, width), BF),...]
where the time goes in v5:
time: 99 us; the launch traced here: 98.9 us
  Pallas kernels  93.4 us (94%)
  local copies, waits for them, and re-layouts  3.59 us (4%)
  other arithmetic  1.1 us (1%)
    pallas_call x1, Pallas kernels, shards(): pl.pallas_call(scatter_kernel, out_shape=(sds((rounds, pad, width), BF),...  38.4 us
    pallas_call x1, Pallas kernels, shards(): pl.pallas_call(gather_kernel, out_shape=(sds((NS, pad, width), BF), sds((...  28.1 us
    pallas_call x1, Pallas kernels, shards(): pl.pallas_call(functools.partial(attention_kernel, scale), out_shape=(sds...  26.6 us
    unnamed x17, local copies, waits for them, and re-layouts  3.47 us

profile of v5, /device:TPU:1, one launch (start us, length us, event | category | flops | bytes accessed | tf_op | source)
XLA Modules:
  0.0 98.9 jit_solution(18148824537495336675)
XLA Ops:
  0.6 0.0 copy-start.6
  0.6 1.0 %copy.23 = bf16[105,4,256]{2,0,1:T(8,128)(2,1)S(1)} copy(bf16[105,4,256]{2,1,0:T(4,128)(2,1)} %param.8) | data formatting | bytes 430080 | tf_op args[0]
  1.7 0.0 copy-start
  1.7 1.1 %copy-done = s32[105,1680]{1,0:T(8,128)S(1)} copy-done((s32[105,1680]{1,0:T(8,128)S(1)}, s32[105,1680]{1,0:T(8,128)}, u32[]{:S(2)}) %copy-start) | copy-done | bytes 705624
  2.8 0.0 copy-start.5
  2.8 0.3 mask_rows.1.b_in
  3.1 0.0 copy-done.6
  3.2 0.0 copy-start.1
  3.2 0.0 copy-start.2
  3.2 0.0 copy-start.3
  3.2 0.0 copy-start.4
  3.2 0.1 copy.22
  3.3 0.2 copy-done.5
  3.5 28.1 %gather.1 = (bf16[16,112,256]{2,1,0:T(8,128)(2,1)S(1)}, bf16[4,112,1792]{2,1,0:T(8,128)(2,1)S(1)}, bf16[4,112,256]{2,1,0:T(8,128)(2,1)S(1)}, f32[4,112,256]{2,1,0:T(8,128)S(1)}) custom-call(bf16[4,112,256]{2,1,0:T(8,128)(2,1)S(1)} %pad.8.x_in, bf16[112,1792]{1,0:T(8,128)(2,1)S(1)} %mask_rows.1.b_in, f32[4,112,256]{2,1,0:T(8,128)S(1)} %pad.9.ct_ref, ...), custom_call_target="tpu_custom_call" | custom-call | tf_op jit(solution)/shard_map/gather/pallas_call | solution.py:463
  31.6 0.0 copy-done.1
  31.6 0.0 copy-done.2
  31.6 0.0 copy-done.3
  31.6 0.0 copy-done.4
  31.6 26.6 %attention.1 = (bf16[1792,256]{1,0:T(8,128)(2,1)S(1)}, f32[8,256,128]{2,1,0:T(8,128)S(1)}) custom-call(bf16[1792,256]{1,0:T(8,128)(2,1)S(1)} %bitcast.31, bf16[448,256]{1,0:T(8,128)(2,1)S(1)} %bitcast.34, bf16[448,1792]{1,0:T(8,128)(2,1)S(1)} %bitcast.30, bf16[256,256]{1,0:T(8,128)(2,1)S(1)} %copy-done.1, bf16[256,256]{1,0:T(8,128)(2,1)S(1)} %copy-done.2, ...), custom_call_target="tpu_custom_call" | custom-call | tf_op jit(solution)/shard_map/attention/pallas_call | solution.py:490
  58.2 38.4 %scatter.1 = (bf16[4,112,256]{2,1,0:T(8,128)(2,1)S(1)}, bf16[8,256,128]{2,1,0:T(8,128)(2,1)S(1)}) custom-call(bf16[16,112,256]{2,1,0:T(8,128)(2,1)S(1)} %bitcast.32, f32[8,256,128]{2,1,0:T(8,128)S(1)} %get-tuple-element.18.g_in), custom_call_target="tpu_custom_call" | custom-call | tf_op jit(solution)/shard_map/scatter/pallas_call | solution.py:525
  96.7 1.0 %copy.17 = f32[105,4,256]{2,1,0:T(4,128)} copy(f32[105,4,256]{2,0,1:T(8,128)S(1)} %fusion) | data formatting | bytes 860160
  97.8 0.1 convert.1
  97.8 0.1 slice_bitcast_fusion
  97.9 1.0 fusion.7
  (3 shorter events, 0.1 us)
Async XLA Ops:
  0.6 2.5 %copy-start.6 = (f32[105,4,256]{2,1,0:T(4,128)S(1)}, f32[105,4,256]{2,1,0:T(4,128)}, u32[]{:S(2)}) copy-start(f32[105,4,256]{2,1,0:T(4,128)} %param.15) | copy-start | bytes 1290244
  1.7 1.1 %copy-start = (s32[105,1680]{1,0:T(8,128)S(1)}, s32[105,1680]{1,0:T(8,128)}, u32[]{:S(2)}) copy-start(s32[105,1680]{1,0:T(8,128)} %mask_ref.1) | copy-start | bytes 2116804
  2.8 0.7 copy-start.5
  3.2 28.4 %copy-start.1 = (bf16[256,256]{1,0:T(8,128)(2,1)S(1)}, bf16[256,256]{1,0:T(8,128)(2,1)}, u32[]{:S(2)}) copy-start(bf16[256,256]{1,0:T(8,128)(2,1)} %wq_ref.1) | copy-start | bytes 393220
  3.2 28.4 %copy-start.2 = (bf16[256,256]{1,0:T(8,128)(2,1)S(1)}, bf16[256,256]{1,0:T(8,128)(2,1)}, u32[]{:S(2)}) copy-start(bf16[256,256]{1,0:T(8,128)(2,1)} %wk_ref.1) | copy-start | bytes 393220
  3.2 28.4 %copy-start.3 = (bf16[256,256]{1,0:T(8,128)(2,1)S(1)}, bf16[256,256]{1,0:T(8,128)(2,1)}, u32[]{:S(2)}) copy-start(bf16[256,256]{1,0:T(8,128)(2,1)} %wv_ref.1) | copy-start | bytes 393220
  3.2 28.4 %copy-start.4 = (bf16[256,256]{1,0:T(8,128)(2,1)S(1)}, bf16[256,256]{1,0:T(8,128)(2,1)}, u32[]{:S(2)}) copy-start(bf16[256,256]{1,0:T(8,128)(2,1)} %wo_ref.1) | copy-start | bytes 393220

commit v6 on v5

--- a/solution.py
+++ b/solution.py
@@ -46,15 +46,6 @@
 
 def nn(a, b):
     return jnp.dot(a, b, preferred_element_type=F32)
-
-
-def mask_kernel(rows, pad, mask_ref, bias_ref):
-    bias_ref[...] = jnp.full(bias_ref.shape, NEG, BF)
-    bias = jnp.where(mask_ref[...] > 0, 0.0, NEG).astype(F32)
-    for group in range(NS):
-        bias_ref[0:rows, group * pad : group * pad + rows] = bias[
-            :, group * rows : (group + 1) * rows
-        ].astype(BF)
 
 
 def attention_kernel(
@@ -186,8 +177,8 @@
 
 
 def gather_kernel(
-    x_in, b_in, ct_ref, decay_ref, x_out, b_out, gb_out, grads_ref,
-    got, late, late_in, gb_send, carried, run, prod, before,
+    rows, x_in, mask_ref, ct_ref, decay_ref, x_out, b_out, gb_out, grads_ref,
+    b_in, got, late, late_in, gb_send, carried, run, prod, before,
     s0, r0, s1, r1, s2, r2, s3, r3, s4, r4, s5, r5, s6, r6, s7, r7, s8, r8, s9, r9, own,
 ):
     rounds, pad, _ = ct_ref.shape
@@ -204,7 +195,6 @@
     upper = t >= NJ
     half = pl.ds(pl.multiple_of(core * cols, cols), cols)
     all_here = greet(False)
-
     level = ct_ref[rounds - 1]
     reach = decay_ref[rounds - 1 : rounds, :]
     for r in range(rounds - 2, -1, -1):
@@ -216,6 +206,13 @@
     d2 = reach - d0 - d1
     row = lax.broadcasted_iota(jnp.int32, (16, reach.shape[1]), 0)
     got[j, pad : pad + 16, :] = jnp.where(row == 0, d0, jnp.where(row == 1, d1, d2)).astype(BF)
+
+    b_in[...] = jnp.full(b_in.shape, NEG, BF)
+    bias = jnp.where(mask_ref[...] > 0, 0.0, NEG).astype(F32)
+    for group in range(NS):
+        b_in[0:rows, group * pad : group * pad + rows] = bias[
+            :, group * rows : (group + 1) * rows
+        ].astype(BF)
 
     all_here()
     scan = []
@@ -249,7 +246,7 @@
         pltpu.make_async_copy(x_in.at[y], x_out.at[me], own.at[0]),
         pltpu.make_async_copy(b_in, b_out.at[y], own.at[1]),
     ]
-    for copy in scan + tokens + list(sides[0]) + masks + local:
+    for copy in list(sides[0]) + tokens + scan + masks + local:
         copy.start()
     for k in range(1, NY):
         tokens[k - 1].wait()
@@ -274,8 +271,8 @@
     late[...] = run[...].astype(BF)
     over = push(late, late_in, (s4, r4), 0, tm=lax.rem(t + NJ, NT))
     pl.when(upper)(over.start)
-    for k in range(2):
-        sides[k][0].wait()
+    for k in range(3):
+        sides[k][0 if k < 2 else 1].wait()
         passed[k].start()
 
     @pl.when(jnp.logical_not(upper))
@@ -297,6 +294,8 @@
     for copy in ups:
         copy.start()
 
+    sides[3][1].wait()
+    passed[3].start()
     shared = []
     for k in range(1, NY):
         masks[k - 1].wait()
@@ -304,9 +303,6 @@
         copy = push(piece, piece, (s5, r5), k, tm=t + 1 - 2 * core)
         copy.start()
         shared.append(copy)
-    for k in range(2, NY):
-        sides[k][1].wait()
-        passed[k].start()
     pl.when(upper)(over.wait_send)
     for copy in (sides[0][1], sides[1][1], sides[2][0], sides[3][0]):
         copy.wait()
@@ -315,7 +311,7 @@
 
 
 def scatter_kernel(
-    c_in, g_in, c_out, g_out, send1, got1, part, got2, send3, got3, got4,
+    c_in, g_in, c_out, g_out, send1, got1, part, send2, got2, send3, got3, got4,
     far_l, far_r, mix_l, mix_r, got_l, got_r, sum_c, s0, r0, s1, r1, s2, r2, s3, r3, s4, r4, s5, r5, s6, r6,
 ):
     me = lax.axis_index("space")
@@ -357,6 +353,20 @@
         push(mix_r, got_l.at[pl.ds(0, two)], (s4, r4), 4, space=right * NY + y),
         push(mix_l, got_r.at[pl.ds(two, two)], (s4, r4), 5, space=left * NY + y),
     ]
+    total = g_in[j]
+    for copy in first:
+        copy.wait()
+    for k in range(1, NJ):
+        total = total + got1[lax.rem(j + k, NJ)].astype(F32)
+    part[...] = total.reshape(part.shape)
+    send2[...] = part[...].astype(send2.dtype)
+
+    second = []
+    for k in range(1, NY):
+        to = lax.rem(y + k, NY)
+        second.append(push(send2.at[to], got2.at[y], (s1, r1), k, space=base + to))
+    for copy in second:
+        copy.start()
     far[0].wait()
     for i in range(two):
         mix_r[i] = (c_in[right * NY + i].astype(F32) + far_l[i].astype(F32)).astype(BF)
@@ -365,24 +375,11 @@
     for i in range(two):
         mix_l[i] = (c_in[left * NY + two + i].astype(F32) + far_r[i].astype(F32)).astype(BF)
     mixed[1].start()
-    total = g_in[j]
-    for copy in first:
-        copy.wait()
-    for k in range(1, NJ):
-        total = total + got1[lax.rem(j + k, NJ)].astype(F32)
-    part[...] = total.reshape(part.shape)
-
-    second = []
-    for k in range(1, NY):
-        to = lax.rem(y + k, NY)
-        second.append(push(part.at[to], got2.at[y], (s1, r1), k, space=base + to))
-    for copy in second:
-        copy.start()
     total = part[y]
     for copy in second:
         copy.wait()
     for k in range(1, NY):
-        total = total + got2[lax.rem(y + k, NY)]
+        total = total + got2[lax.rem(y + k, NY)].astype(F32)
     send3[...] = total.astype(send3.dtype)
     got3[line] = send3[...]
 
@@ -410,18 +407,6 @@
         fourth.append(push(got4.at[y], got4.at[y], (s3, r3), k, space=to))
     for copy in fourth:
         copy.start()
-    for copy in near + mixed:
-        copy.wait()
-    for i in range(NY):
-        block = c_in[z * NY + i].astype(F32) + got_l[i].astype(F32) + got_r[i].astype(F32)
-        sum_c[i] = block.astype(BF)
-    tokens = []
-    for k in range(1, NY):
-        to = lax.rem(y + k, NY)
-        tokens.append(push(sum_c.at[to], c_out.at[y], (s6, r6), k, space=base + to))
-    for copy in tokens:
-        copy.start()
-    c_out[y] = sum_c[y]
     for copy in fourth:
         copy.wait()
     g_out[j] = got4[...].reshape(g_out.shape[1:])
@@ -432,6 +417,18 @@
         fifth.append(push(g_out.at[j], g_out.at[j], (s5, r5), k, tm=to))
     for copy in fifth:
         copy.start()
+    for copy in near + mixed:
+        copy.wait()
+    for i in range(NY):
+        block = c_in[z * NY + i].astype(F32) + got_l[i].astype(F32) + got_r[i].astype(F32)
+        sum_c[i] = block.astype(BF)
+    tokens = []
+    for k in range(1, NY):
+        to = lax.rem(y + k, NY)
+        tokens.append(push(sum_c.at[to], c_out.at[y], (s6, r6), k, space=base + to))
+    for copy in tokens:
+        copy.start()
+    c_out[y] = sum_c[y]
     for copy in fifth + tokens:
         copy.wait()
 
@@ -448,29 +445,22 @@
     size = width // HEADS
     scale = 1.0 / math.sqrt(size)
 
-    bias = pl.pallas_call(
-        functools.partial(mask_kernel, rows, pad),
-        out_shape=sds((pad, keys), BF),
-        in_specs=[VM],
-        out_specs=VM,
-        compiler_params=params(),
-        name="mask_rows",
-    )(mask)
     widen = ((0, 0), (0, pad - rows), (0, 0))
     x = jnp.pad(jnp.swapaxes(tokens, 0, 1), widen)
     ct = jnp.pad(jnp.swapaxes(cotangent, 0, 1), widen)
 
     x_all, bias_all, gb_all, grads = pl.pallas_call(
-        gather_kernel,
+        functools.partial(gather_kernel, rows),
         out_shape=(
             sds((NS, pad, width), BF),
             sds((NY, pad, keys), BF),
             sds((NY, pad, width), BF),
             sds((rounds, pad, width), F32),
         ),
-        in_specs=[ANY, ANY, VM, VM],
+        in_specs=[ANY, VM, VM, VM],
         out_specs=[ANY, ANY, ANY, VM],
         scratch_shapes=[
+            pltpu.VMEM((pad, keys), BF),
             pltpu.VMEM((NJ, pad + 16, width), BF),
             pltpu.VMEM((pad, width), BF),
             pltpu.VMEM((pad, width), BF),
@@ -485,7 +475,7 @@
         ],
         compiler_params=params(cid=1),
         name="gather",
-    )(x, bias, ct, decay)
+    )(x, mask, ct, decay)
 
     c, g = pl.pallas_call(
         functools.partial(attention_kernel, scale),
@@ -531,7 +521,8 @@
             pltpu.VMEM((NJ, 256, 128), wire),
             pltpu.VMEM((NJ, 256, 128), wire),
             pltpu.VMEM((NY, 64, 128), F32),
-            pltpu.VMEM((NY, 64, 128), F32),
+            pltpu.VMEM((NY, 64, 128), wire),
+            pltpu.VMEM((NY, 64, 128), wire),
             pltpu.VMEM((64, 128), wire),
             pltpu.VMEM((NZ, 64, 128), wire),
             pltpu.VMEM((NY, 64, 128), wire),

time: 99 us -> 98.5 us (level)
    pallas_call x1, Pallas kernels: 38.4 us -> 36.8 us  [shards(): pl.pallas_call(scatter_kernel, out_shape=(sds((rounds, pad, width), BF),...]
    pallas_call x2 -> x1, Pallas kernels: 28.4 us -> 29 us  [shards(): pl.pallas_call(functools.partial(gather_kernel, rows), out_shape=(sds((NS...]
    unnamed x17 -> x15, local copies, waits for them, and re-layouts: 3.47 us -> 3.25 us
where the time goes in v6:
time: 98.5 us; the launch traced here: 98.4 us
  Pallas kernels  93.1 us (95%)
  local copies, waits for them, and re-layouts  3.37 us (3%)
  other arithmetic  1.1 us (1%)
    pallas_call x1, Pallas kernels, shards(): pl.pallas_call(scatter_kernel, out_shape=(sds((rounds, pad, width), BF),...  36.8 us
    pallas_call x1, Pallas kernels, shards(): pl.pallas_call(functools.partial(gather_kernel, rows), out_shape=(sds((NS...  29 us
    pallas_call x1, Pallas kernels, shards(): pl.pallas_call(functools.partial(attention_kernel, scale), out_shape=(sds...  27.3 us
    unnamed x15, local copies, waits for them, and re-layouts  3.25 us

profile of v6, /device:TPU:1, one launch (start us, length us, event | category | flops | bytes accessed | tf_op | source)
XLA Modules:
  0.0 98.4 jit_solution(12183947698460515994)
XLA Ops:
  0.6 0.0 copy-start.5
  0.6 0.0 copy-start
  0.7 1.0 %copy.23 = bf16[105,4,256]{2,0,1:T(8,128)(2,1)S(1)} copy(bf16[105,4,256]{2,1,0:T(4,128)(2,1)} %param.8) | data formatting | bytes 430080 | tf_op args[0]
  1.7 0.0 copy-start.1
  1.7 0.0 copy-start.2
  1.7 0.0 copy-start.3
  1.8 0.0 copy-start.4
  1.8 1.1 %copy.22 = f32[105,4,256]{2,0,1:T(8,128)S(1)} copy(f32[105,4,256]{2,1,0:T(4,128)} %param.15) | data formatting | bytes 860160 | tf_op args[7]
  3.0 0.0 copy-done.5
  3.0 0.0 copy-done
  3.0 29.0 %gather.1 = (bf16[16,112,256]{2,1,0:T(8,128)(2,1)S(1)}, bf16[4,112,1792]{2,1,0:T(8,128)(2,1)S(1)}, bf16[4,112,256]{2,1,0:T(8,128)(2,1)S(1)}, f32[4,112,256]{2,1,0:T(8,128)S(1)}) custom-call(bf16[4,112,256]{2,1,0:T(8,128)(2,1)S(1)} %pad.8.x_in, s32[105,1680]{1,0:T(8,128)S(1)} %copy-done, f32[4,112,256]{2,1,0:T(8,128)S(1)} %pad.9.ct_ref, f32[4,256]{1,0:T(4,128)S(1)} %copy-done.5), custom_call_target="tpu_custom_call" | custom-call | tf_op jit(solution)/shard_map/gather/pallas_call | solution.py:452
  32.0 0.0 copy-done.1
  32.0 0.0 copy-done.2
  32.0 0.0 copy-done.3
  32.0 0.0 copy-done.4
  32.0 27.3 %attention.1 = (bf16[1792,256]{1,0:T(8,128)(2,1)S(1)}, f32[8,256,128]{2,1,0:T(8,128)S(1)}) custom-call(bf16[1792,256]{1,0:T(8,128)(2,1)S(1)} %bitcast.31, bf16[448,256]{1,0:T(8,128)(2,1)S(1)} %bitcast.34, bf16[448,1792]{1,0:T(8,128)(2,1)S(1)} %bitcast.30, bf16[256,256]{1,0:T(8,128)(2,1)S(1)} %copy-done.1, bf16[256,256]{1,0:T(8,128)(2,1)S(1)} %copy-done.2, ...), custom_call_target="tpu_custom_call" | custom-call | tf_op jit(solution)/shard_map/attention/pallas_call | solution.py:480
  59.3 36.8 %scatter.1 = (bf16[4,112,256]{2,1,0:T(8,128)(2,1)S(1)}, bf16[8,256,128]{2,1,0:T(8,128)(2,1)S(1)}) custom-call(bf16[16,112,256]{2,1,0:T(8,128)(2,1)S(1)} %bitcast.32, f32[8,256,128]{2,1,0:T(8,128)S(1)} %get-tuple-element.18.g_in), custom_call_target="tpu_custom_call" | custom-call | tf_op jit(solution)/shard_map/scatter/pallas_call | solution.py:515
  96.2 1.0 %copy.17 = f32[105,4,256]{2,1,0:T(4,128)} copy(f32[105,4,256]{2,0,1:T(8,128)S(1)} %fusion) | data formatting | bytes 860160
  97.2 0.1 convert.1
  97.3 0.1 slice_bitcast_fusion
  97.4 1.0 fusion.7
  (3 shorter events, 0.1 us)
Async XLA Ops:
  0.6 2.3 %copy-start.5 = (f32[4,256]{1,0:T(4,128)S(1)}, f32[4,256]{1,0:T(4,128)}, u32[]{:S(2)}) copy-start(f32[4,256]{1,0:T(4,128)} %decay_ref.1) | copy-start | bytes 12292
  0.6 2.3 %copy-start = (s32[105,1680]{1,0:T(8,128)S(1)}, s32[105,1680]{1,0:T(8,128)}, u32[]{:S(2)}) copy-start(s32[105,1680]{1,0:T(8,128)} %mask_ref.1) | copy-start | bytes 2116804
  1.7 30.3 %copy-start.1 = (bf16[256,256]{1,0:T(8,128)(2,1)S(1)}, bf16[256,256]{1,0:T(8,128)(2,1)}, u32[]{:S(2)}) copy-start(bf16[256,256]{1,0:T(8,128)(2,1)} %wq_ref.1) | copy-start | bytes 393220
  1.7 30.3 %copy-start.2 = (bf16[256,256]{1,0:T(8,128)(2,1)S(1)}, bf16[256,256]{1,0:T(8,128)(2,1)}, u32[]{:S(2)}) copy-start(bf16[256,256]{1,0:T(8,128)(2,1)} %wk_ref.1) | copy-start | bytes 393220
  1.7 30.3 %copy-start.3 = (bf16[256,256]{1,0:T(8,128)(2,1)S(1)}, bf16[256,256]{1,0:T(8,128)(2,1)}, u32[]{:S(2)}) copy-start(bf16[256,256]{1,0:T(8,128)(2,1)} %wv_ref.1) | copy-start | bytes 393220
  1.8 30.3 %copy-start.4 = (bf16[256,256]{1,0:T(8,128)(2,1)S(1)}, bf16[256,256]{1,0:T(8,128)(2,1)}, u32[]{:S(2)}) copy-start(bf16[256,256]{1,0:T(8,128)(2,1)} %wo_ref.1) | copy-start | bytes 393220

commit v7 on v6

--- a/solution.py
+++ b/solution.py
@@ -127,7 +127,7 @@
         dvt[here, :] = nn(ut_ref[here, :], pb_ref[...])
         return carry
 
-    lax.fori_loop(0, HEADS, head, 0)
+    lax.fori_loop(0, HEADS, head, 0, unroll=2)
     dq = (acc_q[...] * scale).astype(BF)
     dk = (dkt[...] * scale).astype(BF)
     dv = dvt[...].astype(BF)
@@ -144,6 +144,9 @@
     for i, g in enumerate(weights):
         g_ref[2 * i] = g[:, 0:half]
         g_ref[2 * i + 1] = g[:, half:width]
+
+
+FAR8 = (4, 3, 5, 2, 6, 1, 7)
 
 
 def greet(diagonal):
@@ -216,7 +219,7 @@
 
     all_here()
     scan = []
-    for k in range(1, NJ):
+    for k in FAR8:
         to = t - j + lax.rem(j + k, NJ)
         scan.append(push(got.at[j], got.at[j], (s3, r3), k, tm=to))
     tokens = []
@@ -329,7 +332,7 @@
     all_here()
 
     first = []
-    for k in range(1, NJ):
+    for k in FAR8:
         to = lax.rem(j + k, NJ)
         first.append(push(send1.at[to], got1.at[j], (s0, r0), k, tm=t - j + to))
     two = 2
@@ -384,7 +387,7 @@
     got3[line] = send3[...]
 
     third = []
-    for k in range(1, NZ):
+    for k in FAR8:
         to = lax.rem(line + k, NZ)
         third.append(
             push(
@@ -412,7 +415,7 @@
     g_out[j] = got4[...].reshape(g_out.shape[1:])
 
     fifth = []
-    for k in range(1, NJ):
+    for k in FAR8:
         to = t - j + lax.rem(j + k, NJ)
         fifth.append(push(g_out.at[j], g_out.at[j], (s5, r5), k, tm=to))
     for copy in fifth:

time: 98.5 us -> 96.1 us (0.976)
  Pallas kernels: 93.1 us -> 90.7 us
    pallas_call x1, Pallas kernels: 36.8 us -> 35.6 us  [shards(): pl.pallas_call(scatter_kernel, out_shape=(sds((rounds, pad, width), BF),...]
where the time goes in v7:
time: 96.1 us; the launch traced here: 96 us
  Pallas kernels  90.7 us (94%)
  local copies, waits for them, and re-layouts  3.37 us (4%)
  other arithmetic  1.1 us (1%)
    pallas_call x1, Pallas kernels, shards(): pl.pallas_call(scatter_kernel, out_shape=(sds((rounds, pad, width), BF),...  35.6 us
    pallas_call x1, Pallas kernels, shards(): pl.pallas_call(functools.partial(gather_kernel, rows), out_shape=(sds((NS...  28.5 us
    pallas_call x1, Pallas kernels, shards(): pl.pallas_call(functools.partial(attention_kernel, scale), out_shape=(sds...  26.7 us
    unnamed x15, local copies, waits for them, and re-layouts  3.25 us

profile of v7, /device:TPU:1, one launch (start us, length us, event | category | flops | bytes accessed | tf_op | source)
XLA Modules:
  0.0 96.0 jit_solution(1654965353404947590)
XLA Ops:
  0.6 0.0 copy-start.5
  0.6 0.0 copy-start
  0.7 1.0 %copy.23 = bf16[105,4,256]{2,0,1:T(8,128)(2,1)S(1)} copy(bf16[105,4,256]{2,1,0:T(4,128)(2,1)} %param.8) | data formatting | bytes 430080 | tf_op args[0]
  1.7 0.0 copy-start.1
  1.7 0.0 copy-start.2
  1.7 0.0 copy-start.3
  1.8 0.0 copy-start.4
  1.8 1.1 %copy.22 = f32[105,4,256]{2,0,1:T(8,128)S(1)} copy(f32[105,4,256]{2,1,0:T(4,128)} %param.15) | data formatting | bytes 860160 | tf_op args[7]
  3.0 0.0 copy-done.5
  3.0 0.0 copy-done
  3.0 28.5 %gather.1 = (bf16[16,112,256]{2,1,0:T(8,128)(2,1)S(1)}, bf16[4,112,1792]{2,1,0:T(8,128)(2,1)S(1)}, bf16[4,112,256]{2,1,0:T(8,128)(2,1)S(1)}, f32[4,112,256]{2,1,0:T(8,128)S(1)}) custom-call(bf16[4,112,256]{2,1,0:T(8,128)(2,1)S(1)} %pad.8.x_in, s32[105,1680]{1,0:T(8,128)S(1)} %copy-done, f32[4,112,256]{2,1,0:T(8,128)S(1)} %pad.9.ct_ref, f32[4,256]{1,0:T(4,128)S(1)} %copy-done.5), custom_call_target="tpu_custom_call" | custom-call | tf_op jit(solution)/shard_map/gather/pallas_call | solution.py:455
  31.4 0.0 copy-done.1
  31.5 0.0 copy-done.2
  31.5 0.0 copy-done.3
  31.5 0.0 copy-done.4
  31.5 26.7 %attention.1 = (bf16[1792,256]{1,0:T(8,128)(2,1)S(1)}, f32[8,256,128]{2,1,0:T(8,128)S(1)}) custom-call(bf16[1792,256]{1,0:T(8,128)(2,1)S(1)} %bitcast.31, bf16[448,256]{1,0:T(8,128)(2,1)S(1)} %bitcast.34, bf16[448,1792]{1,0:T(8,128)(2,1)S(1)} %bitcast.30, bf16[256,256]{1,0:T(8,128)(2,1)S(1)} %copy-done.1, bf16[256,256]{1,0:T(8,128)(2,1)S(1)} %copy-done.2, ...), custom_call_target="tpu_custom_call" | custom-call | tf_op jit(solution)/shard_map/attention/pallas_call | solution.py:483
  58.2 35.6 %scatter.1 = (bf16[4,112,256]{2,1,0:T(8,128)(2,1)S(1)}, bf16[8,256,128]{2,1,0:T(8,128)(2,1)S(1)}) custom-call(bf16[16,112,256]{2,1,0:T(8,128)(2,1)S(1)} %bitcast.32, f32[8,256,128]{2,1,0:T(8,128)S(1)} %get-tuple-element.18.g_in), custom_call_target="tpu_custom_call" | custom-call | tf_op jit(solution)/shard_map/scatter/pallas_call | solution.py:518
  93.8 1.0 %copy.17 = f32[105,4,256]{2,1,0:T(4,128)} copy(f32[105,4,256]{2,0,1:T(8,128)S(1)} %fusion) | data formatting | bytes 860160
  94.8 0.1 convert.1
  94.9 0.1 slice_bitcast_fusion
  95.0 1.0 %fusion.7 = (f32[256,256]{1,0:T(8,128)}, f32[256,256]{1,0:T(8,128)}, f32[256,256]{1,0:T(8,128)}, f32[256,256]{1,0:T(8,128)}) fusion(f32[4,256,128]{2,1,0:T(8,128)S(1)} %get-tuple-element.30, f32[4,256,128]{2,1,0:T(8,128)S(1)} %get-tuple-element.31), kind=kLoop, calls=%fused_computation.18 | loop fusion | flops 262144 | bytes 2097152 | tf_op jit(solution)/shard_map/squeeze | solution.py:549
  (3 shorter events, 0.1 us)
Async XLA Ops:
  0.6 2.3 %copy-start.5 = (f32[4,256]{1,0:T(4,128)S(1)}, f32[4,256]{1,0:T(4,128)}, u32[]{:S(2)}) copy-start(f32[4,256]{1,0:T(4,128)} %decay_ref.1) | copy-start | bytes 12292
  0.6 2.3 %copy-start = (s32[105,1680]{1,0:T(8,128)S(1)}, s32[105,1680]{1,0:T(8,128)}, u32[]{:S(2)}) copy-start(s32[105,1680]{1,0:T(8,128)} %mask_ref.1) | copy-start | bytes 2116804
  1.7 29.7 %copy-start.1 = (bf16[256,256]{1,0:T(8,128)(2,1)S(1)}, bf16[256,256]{1,0:T(8,128)(2,1)}, u32[]{:S(2)}) copy-start(bf16[256,256]{1,0:T(8,128)(2,1)} %wq_ref.1) | copy-start | bytes 393220
  1.7 29.7 %copy-start.2 = (bf16[256,256]{1,0:T(8,128)(2,1)S(1)}, bf16[256,256]{1,0:T(8,128)(2,1)}, u32[]{:S(2)}) copy-start(bf16[256,256]{1,0:T(8,128)(2,1)} %wk_ref.1) | copy-start | bytes 393220
  1.7 29.7 %copy-start.3 = (bf16[256,256]{1,0:T(8,128)(2,1)S(1)}, bf16[256,256]{1,0:T(8,128)(2,1)}, u32[]{:S(2)}) copy-start(bf16[256,256]{1,0:T(8,128)(2,1)} %wv_ref.1) | copy-start | bytes 393220
  1.8 29.7 %copy-start.4 = (bf16[256,256]{1,0:T(8,128)(2,1)S(1)}, bf16[256,256]{1,0:T(8,128)(2,1)}, u32[]{:S(2)}) copy-start(bf16[256,256]{1,0:T(8,128)(2,1)} %wo_ref.1) | copy-start | bytes 393220

commit v8 on v7

--- a/solution.py
+++ b/solution.py
@@ -127,7 +127,7 @@
         dvt[here, :] = nn(ut_ref[here, :], pb_ref[...])
         return carry
 
-    lax.fori_loop(0, HEADS, head, 0, unroll=2)
+    lax.fori_loop(0, HEADS, head, 0, unroll=4)
     dq = (acc_q[...] * scale).astype(BF)
     dk = (dkt[...] * scale).astype(BF)
     dv = dvt[...].astype(BF)
@@ -365,7 +365,7 @@
     send2[...] = part[...].astype(send2.dtype)
 
     second = []
-    for k in range(1, NY):
+    for k in (2, 1, 3):
         to = lax.rem(y + k, NY)
         second.append(push(send2.at[to], got2.at[y], (s1, r1), k, space=base + to))
     for copy in second:
@@ -405,7 +405,7 @@
     got4[y] = total.astype(got4.dtype)
 
     fourth = []
-    for k in range(1, NY):
+    for k in (2, 1, 3):
         to = base + lax.rem(y + k, NY)
         fourth.append(push(got4.at[y], got4.at[y], (s3, r3), k, space=to))
     for copy in fourth:

time: 96.1 us -> 95.4 us (level)
  no operation moved by 1% of the time
where the time goes in v8:
time: 95.4 us; the launch traced here: 95.3 us
  Pallas kernels  90 us (94%)
  local copies, waits for them, and re-layouts  3.37 us (4%)
  other arithmetic  1.1 us (1%)
    pallas_call x1, Pallas kernels, shards(): pl.pallas_call(scatter_kernel, out_shape=(sds((rounds, pad, width), BF),...  34.9 us
    pallas_call x1, Pallas kernels, shards(): pl.pallas_call(functools.partial(gather_kernel, rows), out_shape=(sds((NS...  28.5 us
    pallas_call x1, Pallas kernels, shards(): pl.pallas_call(functools.partial(attention_kernel, scale), out_shape=(sds...  26.6 us
    unnamed x15, local copies, waits for them, and re-layouts  3.25 us

profile of v8, /device:TPU:1, one launch (start us, length us, event | category | flops | bytes accessed | tf_op | source)
XLA Modules:
  0.0 95.3 jit_solution(6339185434447173123)
XLA Ops:
  0.6 0.0 copy-start.5
  0.6 0.0 copy-start
  0.7 1.0 %copy.23 = bf16[105,4,256]{2,0,1:T(8,128)(2,1)S(1)} copy(bf16[105,4,256]{2,1,0:T(4,128)(2,1)} %param.8) | data formatting | bytes 430080 | tf_op args[0]
  1.7 0.0 copy-start.1
  1.7 0.0 copy-start.2
  1.7 0.0 copy-start.3
  1.8 0.0 copy-start.4
  1.8 1.1 %copy.22 = f32[105,4,256]{2,0,1:T(8,128)S(1)} copy(f32[105,4,256]{2,1,0:T(4,128)} %param.15) | data formatting | bytes 860160 | tf_op args[7]
  3.0 0.0 copy-done.5
  3.0 0.0 copy-done
  3.0 28.5 %gather.1 = (bf16[16,112,256]{2,1,0:T(8,128)(2,1)S(1)}, bf16[4,112,1792]{2,1,0:T(8,128)(2,1)S(1)}, bf16[4,112,256]{2,1,0:T(8,128)(2,1)S(1)}, f32[4,112,256]{2,1,0:T(8,128)S(1)}) custom-call(bf16[4,112,256]{2,1,0:T(8,128)(2,1)S(1)} %pad.8.x_in, s32[105,1680]{1,0:T(8,128)S(1)} %copy-done, f32[4,112,256]{2,1,0:T(8,128)S(1)} %pad.9.ct_ref, f32[4,256]{1,0:T(4,128)S(1)} %copy-done.5), custom_call_target="tpu_custom_call" | custom-call | tf_op jit(solution)/shard_map/gather/pallas_call | solution.py:455
  31.4 0.0 copy-done.1
  31.5 0.0 copy-done.2
  31.5 0.0 copy-done.3
  31.5 0.0 copy-done.4
  31.5 26.6 %attention.1 = (bf16[1792,256]{1,0:T(8,128)(2,1)S(1)}, f32[8,256,128]{2,1,0:T(8,128)S(1)}) custom-call(bf16[1792,256]{1,0:T(8,128)(2,1)S(1)} %bitcast.31, bf16[448,256]{1,0:T(8,128)(2,1)S(1)} %bitcast.34, bf16[448,1792]{1,0:T(8,128)(2,1)S(1)} %bitcast.30, bf16[256,256]{1,0:T(8,128)(2,1)S(1)} %copy-done.1, bf16[256,256]{1,0:T(8,128)(2,1)S(1)} %copy-done.2, ...), custom_call_target="tpu_custom_call" | custom-call | tf_op jit(solution)/shard_map/attention/pallas_call | solution.py:483
  58.1 34.9 %scatter.1 = (bf16[4,112,256]{2,1,0:T(8,128)(2,1)S(1)}, bf16[8,256,128]{2,1,0:T(8,128)(2,1)S(1)}) custom-call(bf16[16,112,256]{2,1,0:T(8,128)(2,1)S(1)} %bitcast.32, f32[8,256,128]{2,1,0:T(8,128)S(1)} %get-tuple-element.18.g_in), custom_call_target="tpu_custom_call" | custom-call | tf_op jit(solution)/shard_map/scatter/pallas_call | solution.py:518
  93.1 1.0 %copy.17 = f32[105,4,256]{2,1,0:T(4,128)} copy(f32[105,4,256]{2,0,1:T(8,128)S(1)} %fusion) | data formatting | bytes 860160
  94.2 0.1 convert.1
  94.2 0.1 slice_bitcast_fusion
  94.3 1.0 %fusion.7 = (f32[256,256]{1,0:T(8,128)}, f32[256,256]{1,0:T(8,128)}, f32[256,256]{1,0:T(8,128)}, f32[256,256]{1,0:T(8,128)}) fusion(f32[4,256,128]{2,1,0:T(8,128)S(1)} %get-tuple-element.30, f32[4,256,128]{2,1,0:T(8,128)S(1)} %get-tuple-element.31), kind=kLoop, calls=%fused_computation.18 | loop fusion | flops 262144 | bytes 2097152 | tf_op jit(solution)/shard_map/squeeze | solution.py:549
  (3 shorter events, 0.1 us)
Async XLA Ops:
  0.6 2.3 %copy-start.5 = (f32[4,256]{1,0:T(4,128)S(1)}, f32[4,256]{1,0:T(4,128)}, u32[]{:S(2)}) copy-start(f32[4,256]{1,0:T(4,128)} %decay_ref.1) | copy-start | bytes 12292
  0.6 2.3 %copy-start = (s32[105,1680]{1,0:T(8,128)S(1)}, s32[105,1680]{1,0:T(8,128)}, u32[]{:S(2)}) copy-start(s32[105,1680]{1,0:T(8,128)} %mask_ref.1) | copy-start | bytes 2116804
  1.7 29.7 %copy-start.1 = (bf16[256,256]{1,0:T(8,128)(2,1)S(1)}, bf16[256,256]{1,0:T(8,128)(2,1)}, u32[]{:S(2)}) copy-start(bf16[256,256]{1,0:T(8,128)(2,1)} %wq_ref.1) | copy-start | bytes 393220
  1.7 29.7 %copy-start.2 = (bf16[256,256]{1,0:T(8,128)(2,1)S(1)}, bf16[256,256]{1,0:T(8,128)(2,1)}, u32[]{:S(2)}) copy-start(bf16[256,256]{1,0:T(8,128)(2,1)} %wk_ref.1) | copy-start | bytes 393220
  1.7 29.7 %copy-start.3 = (bf16[256,256]{1,0:T(8,128)(2,1)S(1)}, bf16[256,256]{1,0:T(8,128)(2,1)}, u32[]{:S(2)}) copy-start(bf16[256,256]{1,0:T(8,128)(2,1)} %wv_ref.1) | copy-start | bytes 393220
  1.8 29.7 %copy-start.4 = (bf16[256,256]{1,0:T(8,128)(2,1)S(1)}, bf16[256,256]{1,0:T(8,128)(2,1)}, u32[]{:S(2)}) copy-start(bf16[256,256]{1,0:T(8,128)(2,1)} %wo_ref.1) | copy-start | bytes 393220
